TPU v7x, 512 devices: a whole 4x4x16 slice. The times are simulated.
512 devices in a mesh: gx: 64 (over z, y), gy: 8 (over x, core).
Axes of the slice: x: 4, y: 4, z: 16, core: 2. Of those that a mesh axis runs over, the one named last changes fastest.
Arguments:
- velocity: float32 [3, 256, 64, 256], P(None, 'gx', 'gy'), may hold values from -6 to 6
- cotangent: float32 [3, 256, 64, 256], P(None, 'gx', 'gy'), may hold values from -10.5 to 13.5
- weight_in: float32 [6, 64], replicated, may hold values from -2.5 to 2.5
- bias_in: float32 [64], replicated, may hold values from -3 to 3
- weight_out: float32 [64, 3], replicated, may hold values from -0.75 to 0.75
Outputs:
- new_velocity: float32 [3, 256, 64, 256], P(None, 'gx', 'gy')
- grad_velocity: float32 [3, 256, 64, 256], P(None, 'gx', 'gy')
- grad_weight_in: float32 [6, 64], replicated
- grad_bias_in: float32 [64], replicated
- grad_weight_out: float32 [64, 3], replicated
All inputs are finite; a program needn't handle non-finite values.
Results may differ from a plain program's by a relative error of at most 0.0003.
Values sent between devices are 32-bit elements; how exact they have to be, the bound alone decides.
A program may use at most 64 MiB of HBM per device.

v0:
```python
import jax
import jax.numpy as jnp
import numpy as np
from jax import lax
from jax.sharding import PartitionSpec as P

FILTER_ALPHA = 0.499
FILTER_GAIN = 0.5 + FILTER_ALPHA
COMPACT_ALPHA = 1.0 / 3.0
STEP_SIZE = 0.5
PRECISE = lax.Precision.HIGHEST


def extended(array, sides, width):
    for axis, dim in sides:
        devices, length = (lax.axis_size(axis), array.shape[dim])
        up = [(i, (i + 1) % devices) for i in range(devices - 1)]
        down = [(j, i) for i, j in up]
        last = lax.slice_in_dim(array, length - width, length, axis=dim)
        leading = lax.slice_in_dim(array, 0, width, axis=dim)
        before = lax.ppermute(last, axis, up)
        after = lax.ppermute(leading, axis, down)
        array = jnp.concatenate([before, array, after], axis=dim)
    return array


def carried_in(part, axis, combine, identity, reverse):
    count = lax.axis_size(axis)
    place = lax.axis_index(axis)
    ahead = count - 1 - place if reverse else place
    gathered = jax.tree.map(lambda a: lax.all_gather(a, axis), part)
    state = jax.tree.map(lambda a, e: jnp.zeros_like(a) + jnp.asarray(e, a.dtype), part, identity)

    def one(turn, state):
        source = count - 1 - turn if reverse else turn
        return combine(
            state, jax.tree.map(lambda a: lax.dynamic_index_in_dim(a, source, 0, False), gathered)
        )

    return lax.fori_loop(0, ahead, one, state)


def derivative_table(length):
    weights = 7.0 / 9.0 * (np.eye(length, k=1) - np.eye(length, k=-1)) + 1.0 / 36.0 * (
        np.eye(length, k=2) - np.eye(length, k=-2)
    )
    uppers = np.zeros(length)
    before = 0.0
    previous = np.zeros(length)
    for position in range(length):
        scale = 1.0 / (1.0 - COMPACT_ALPHA * before)
        weights[position] = (weights[position] - COMPACT_ALPHA * previous) * scale
        before = COMPACT_ALPHA * scale
        uppers[position] = before
        previous = weights[position]
    for position in reversed(range(length - 1)):
        weights[position] = weights[position] - uppers[position] * weights[position + 1]
    return weights.astype(np.float32)


def sweep_tables(length):
    scales = np.zeros(length)
    uppers = np.zeros(length)
    before = 0.0
    for position in range(length):
        scales[position] = 1.0 / (1.0 - FILTER_ALPHA * before)
        before = FILTER_ALPHA * scales[position]
        uppers[position] = before
    return (scales.astype(np.float32), uppers.astype(np.float32))


def combine(earlier, later):
    return (earlier[0] * later[0], later[0] * earlier[1] + later[1])


def smooth_x(values):
    x_rows = values.shape[1]
    scales_all, uppers_all = sweep_tables(x_rows * lax.axis_size("gx"))
    offset = lax.axis_index("gx") * x_rows
    scales = lax.dynamic_slice_in_dim(jnp.asarray(scales_all), offset, x_rows)
    uppers = lax.dynamic_slice_in_dim(jnp.asarray(uppers_all), offset, x_rows)
    padded = extended(values, (("gx", 1),), 1)
    right_side = FILTER_GAIN * values + 0.5 * FILTER_GAIN * (padded[:, :-2] + padded[:, 2:])
    previous = jnp.zeros_like(values[:, 0])
    factor = jnp.ones((1, 1), jnp.float32)
    partial_rows = []
    factors = []
    for row_index in range(x_rows):
        previous = (right_side[:, row_index] - FILTER_ALPHA * previous) * scales[row_index]
        factor = factor * (-FILTER_ALPHA * scales[row_index])
        partial_rows.append(previous)
        factors.append(factor)
    identity = (jnp.ones((1, 1), jnp.float32), jnp.zeros_like(previous))
    incoming = carried_in((factor, previous), "gx", combine, identity, False)
    eliminated = [
        partial_rows[row_index] + factors[row_index] * incoming[1] for row_index in range(x_rows)
    ]
    following = jnp.zeros_like(previous)
    factor = jnp.ones((1, 1), jnp.float32)
    solved_rows = [None] * x_rows
    back_factors = [None] * x_rows
    for row_index in reversed(range(x_rows)):
        following = eliminated[row_index] - uppers[row_index] * following
        factor = factor * -uppers[row_index]
        solved_rows[row_index] = following
        back_factors[row_index] = factor
    upper_value = carried_in((factor, following), "gx", combine, identity, True)
    finished = [
        solved_rows[row_index] + back_factors[row_index] * upper_value[1]
        for row_index in range(x_rows)
    ]
    return jnp.stack(finished, axis=1)


def y_pass(values, table):
    derived = jnp.einsum(
        "ab,kxbz->kxaz",
        table,
        lax.all_to_all(values, "gy", split_axis=3, concat_axis=2, tiled=True),
        precision=PRECISE,
    )
    return lax.all_to_all(derived, "gy", split_axis=2, concat_axis=3, tiled=True)


def closure_plane(feature_plane, cotangent_plane, weight_in, bias_in, weight_out):
    pre = jnp.dot(weight_in.T, feature_plane, precision=PRECISE) + bias_in[:, None]
    hidden = jnp.tanh(pre)
    forcing = jnp.dot(weight_out.T, hidden, precision=PRECISE)
    grad_out = STEP_SIZE * cotangent_plane
    grad_hidden = jnp.dot(weight_out, grad_out, precision=PRECISE)
    grad_pre = grad_hidden * (1.0 - hidden * hidden)
    grad_feature = jnp.dot(weight_in, grad_pre, precision=PRECISE)
    sum_in = jnp.dot(feature_plane, grad_pre.T, precision=PRECISE)
    sum_bias = jnp.sum(grad_pre, axis=1)
    sum_out = jnp.dot(hidden, grad_out.T, precision=PRECISE)
    return (forcing, grad_feature, sum_in, sum_bias, sum_out)


def local(velocity, cotangent, weight_in, bias_in, weight_out):
    x_rows = velocity.shape[1]
    y_rows = velocity.shape[2]
    z_length = velocity.shape[3]
    y_length = y_rows * lax.axis_size("gy")
    y_table = jnp.asarray(derivative_table(y_length))
    z_table = jnp.asarray(derivative_table(z_length))
    smoothed = smooth_x(velocity)
    along_z = jnp.einsum("ab,kxyb->kxya", z_table, smoothed, precision=PRECISE)
    along_y = y_pass(smoothed, y_table)
    features = jnp.concatenate([along_y, along_z], axis=0)
    plane_cells = y_rows * z_length
    forcing_rows = []
    gradient_rows = []
    sum_in = jnp.zeros((6, weight_in.shape[1]), jnp.float32)
    sum_bias = jnp.zeros((weight_in.shape[1],), jnp.float32)
    sum_out = jnp.zeros((weight_in.shape[1], 3), jnp.float32)
    for row_index in range(x_rows):
        feature_plane = features[:, row_index].reshape(6, plane_cells)
        cotangent_plane = cotangent[:, row_index].reshape(3, plane_cells)
        forcing, grad_feature, part_in, part_bias, part_out = closure_plane(
            feature_plane, cotangent_plane, weight_in, bias_in, weight_out
        )
        forcing_rows.append(forcing.reshape(3, y_rows, z_length))
        gradient_rows.append(grad_feature.reshape(6, y_rows, z_length))
        sum_in = sum_in + part_in
        sum_bias = sum_bias + part_bias
        sum_out = sum_out + part_out
    new_velocity = velocity + STEP_SIZE * jnp.stack(forcing_rows, axis=1)
    grad_features = jnp.stack(gradient_rows, axis=1)
    back_y = y_pass(grad_features[0:3], y_table.T)
    back_z = jnp.einsum("ba,kxyb->kxya", z_table, grad_features[3:6], precision=PRECISE)
    grad_velocity = cotangent + smooth_x(back_y + back_z)
    totals = lax.psum((sum_in, sum_bias, sum_out), ("gx", "gy"))
    cells = float(x_rows * lax.axis_size("gx") * y_length * z_length)
    return (new_velocity, grad_velocity, totals[0] / cells, totals[1] / cells, totals[2] / cells)


def solution(mesh):
    in_specs = (P(None, "gx", "gy", None), P(None, "gx", "gy", None), P(), P(), P())
    out_specs = (P(None, "gx", "gy", None), P(None, "gx", "gy", None), P(), P(), P())
    return jax.shard_map(local, mesh=mesh, in_specs=in_specs, out_specs=out_specs, check_vma=False)
```

profile of v0, /device:TPU:2, one launch (start us, length us, event | category | flops | bytes accessed | tf_op | source)
XLA Modules:
  0.0 1216.4 jit_solution(16932506660493872590)
XLA Ops:
  8.0 3.5 collective-permute-start
  15.1 2.1 collective-permute-done.1
  17.2 3.0 multiply_bitcast_fusion.1
  30.8 149.0 %all-reduce.3 = (f32[64]{0:T(128)S(1)}, f32[64]{0:T(128)S(1)}) all-reduce(f32[64]{0:T(128)S(1)} %dynamic-update-slice.1, f32[64]{0:T(128)S(1)} %dynamic-update-slice), channel_id=1, replica_groups=mesh['gx'=64,'gy'=8] {'gx'}, use_global_device_ids=true, to_apply=%add.1 | all-reduce | flops 128 | bytes 1024
  179.9 4.9 fusion.30
  184.8 252.8 %all-gather.9.cloned.1.call-done = f32[192,8,256]{2,1,0:T(8,128)} async-done(((f32[3,8,256]{2,1,0:T(8,128)}), f32[192,8,256]{2,1,0:T(8,128)}) %all-gather.9.cloned.1.call-update) | async-done | bytes 1572880 | tf_op jit(solution)/shard_map/all_gather | solution.py:31
  437.6 124.3 %while.53 = (s32[]{:T(128)}, f32[3,8,256]{2,1,0:T(8,128)S(1)}, s32[]{:T(128)}, f32[64,1,1]{0,2,1:T(1,128)S(1)}, f32[64,3,8,256]{3,2,1,0:T(8,128)}, /*index=5*/s32[]{:T(128)}, s32[]{:T(128)}, s32[]{:T(128)}, s32[]{:T(128)}) while((s32[]{:T(128)}, f32[3,8,256]{2,1,0:T(8,128)S(1)}, s32[]{:T(128)}, f32[64,1,1]{0,2,1:T(1,128)S(1)}, ...), condition=%wide.region_3.4_spmd, body=%wide.region_2.3_spmd.sunk | while | flops 12294 | bytes 73895 | solution.py:40
  438.2 1.4 bitcast_add_fusion.11
  440.2 1.4 bitcast_add_fusion.11
  442.1 1.4 bitcast_add_fusion.11
  444.1 1.4 bitcast_add_fusion.11
  446.1 1.4 bitcast_add_fusion.11
  448.0 1.4 bitcast_add_fusion.11
  450.0 1.4 bitcast_add_fusion.11
  452.0 1.4 bitcast_add_fusion.11
  454.0 1.4 bitcast_add_fusion.11
  457.9 1.4 bitcast_add_fusion.11
  459.9 1.4 bitcast_add_fusion.11
  461.9 1.4 bitcast_add_fusion.11
  463.8 1.4 bitcast_add_fusion.11
  465.8 1.4 bitcast_add_fusion.11
  467.8 1.4 bitcast_add_fusion.11
  469.8 1.4 bitcast_add_fusion.11
  471.7 1.4 bitcast_add_fusion.11
  473.7 1.4 bitcast_add_fusion.11
  475.7 1.4 bitcast_add_fusion.11
  477.6 1.4 bitcast_add_fusion.11
  479.6 1.4 bitcast_add_fusion.11
  481.6 1.4 bitcast_add_fusion.11
  483.6 1.4 bitcast_add_fusion.11
  485.5 1.4 bitcast_add_fusion.11
  487.5 1.4 bitcast_add_fusion.11
  489.5 1.4 bitcast_add_fusion.11
  491.5 1.4 bitcast_add_fusion.11
  495.4 1.4 bitcast_add_fusion.11
  497.4 1.4 bitcast_add_fusion.11
  499.4 1.4 bitcast_add_fusion.11
  501.3 1.4 bitcast_add_fusion.11
  503.3 1.4 bitcast_add_fusion.11
  505.3 1.4 bitcast_add_fusion.11
  561.9 2.5 add_bitcast_fusion.6
  565.2 2.4 reshape.250
  567.6 4.8 all-to-all-start
  572.6 4.2 all-to-all-done
  578.2 1.9 reshape.251
  582.7 4.7 all-to-all-start.1
  587.8 4.0 all-to-all-done.1
  603.9 1.5 copy.85
  605.4 3.2 reshape.254
  608.6 8.2 all_to_all.72
  617.6 3.1 reshape.255
  620.7 2.2 copy.86
  623.9 2.2 convolution_bitcast_fusion
  628.2 9.1 all_to_all.73
  637.3 1.5 reduce.7
  644.9 4.2 collective-permute-done.3
  649.2 3.0 multiply_bitcast_fusion
  656.0 124.5 %all-gather.15.cloned.1.call-done = f32[192,1,8,256]{3,2,1,0:T(8,128)} async-done(((f32[3,1,8,256]{3,2,1,0:T(8,128)}), f32[192,1,8,256]{3,2,1,0:T(8,128)}) %all-gather.15.cloned.1.call-update) | async-done | bytes 1572880 | tf_op jit(solution)/shard_map/all_gather | solution.py:31
  780.6 4.9 fusion.24
  787.3 1.6 convolution_add_fusion.5
  788.9 262.2 %all-reduce.2 = (f32[6,64]{1,0:T(8,128)S(1)}, f32[64]{0:T(128)S(1)}, f32[64,3]{0,1:T(4,128)S(1)}) all-reduce(f32[6,64]{1,0:T(8,128)S(1)} %convolution_add_fusion.5, f32[64]{0:T(128)S(1)} %add_add_fusion, f32[64,3]{0,1:T(4,128)S(1)} %convolution_add_fusion.8), channel_id=1, replica_groups=mesh['gx'=64,'gy'=8] {'gx','gy'}, use_global_device_ids=true, to_apply=%region_8.9 | all-reduce | flops 640 | bytes 5120 | tf_op jit(solution)/shard_map/psum | solution.py:172
  1055.1 25.8 %all-gather.11.cloned.1.call-done = f32[192,8,256]{2,1,0:T(8,128)} async-done(((f32[3,8,256]{2,1,0:T(8,128)}), f32[192,8,256]{2,1,0:T(8,128)}) %all-gather.11.cloned.1.call-update) | async-done | bytes 1572880 | tf_op jit(solution)/shard_map/all_gather | solution.py:31
  1080.9 126.5 %while.55 = (s32[]{:T(128)}, f32[3,8,256]{2,1,0:T(8,128)S(1)}, s32[]{:T(128)}, f32[64,1,1]{0,2,1:T(1,128)S(1)}, f32[64,3,8,256]{3,2,1,0:T(8,128)}, /*index=5*/s32[]{:T(128)}, s32[]{:T(128)}, s32[]{:T(128)}, s32[]{:T(128)}) while((s32[]{:T(128)}, f32[3,8,256]{2,1,0:T(8,128)S(1)}, s32[]{:T(128)}, f32[64,1,1]{0,2,1:T(1,128)S(1)}, ...), condition=%wide.region_7.8_spmd, body=%wide.region_6.7_spmd.sunk | while | flops 12294 | bytes 73895 | solution.py:40
  1207.4 1.8 add_bitcast_fusion.2
  (383 shorter events, 250.7 us)
Async XLA Ops:
  7.2 586.2 %copy-start = (f32[6,64]{1,0:T(8,128)S(1)}, f32[6,64]{1,0:T(8,128)}, u32[]{:S(2)}) copy-start(f32[6,64]{1,0:T(8,128)} %param.21) | copy-start | bytes 4612
  7.2 172.6 %all-gather.13.cloned.1.call-start = ((), (), s32[]{:S(2)}) async-start(), calls=%async_computation.6 | async-start | bytes 1597440 | tf_op jit(solution)/shard_map/all_gather | solution.py:31
  8.0 7.1 collective-permute-start
  11.5 5.7 collective-permute-start.1
  20.3 417.3 %all-gather.9.cloned.1.call-start = ((), (), s32[]{:S(2)}) async-start(), calls=%async_computation.4 | async-start | bytes 1597440 | tf_op jit(solution)/shard_map/all_gather | solution.py:31
  179.9 257.7 %copy-start.29 = (f32[64,1,1]{0,2,1:T(1,128)}, f32[64,1,1]{0,2,1:T(1,128)S(1)}, u32[]{:S(2)}) copy-start(f32[64,1,1]{0,2,1:T(1,128)S(1)} %get-tuple-element.634) | copy-start | bytes 772
  561.9 2.5 copy-start.27
  564.4 8.0 copy-start.13
  567.6 9.2 all-to-all-start
  572.5 28.2 %copy-start.19 = (f32[1,3,8,256]{3,1,2,0:T(4,128)}, f32[1,3,8,256]{3,1,2,0:T(4,128)S(1)}, u32[]{:S(2)}) copy-start(f32[1,3,8,256]{3,1,2,0:T(4,128)S(1)} %copy.110) | copy-start | bytes 73732
  572.5 24.8 %copy-start.15 = (f32[1,3,8,256]{3,1,2,0:T(4,128)}, f32[1,3,8,256]{3,1,2,0:T(4,128)S(1)}, u32[]{:S(2)}) copy-start(f32[1,3,8,256]{3,1,2,0:T(4,128)S(1)} %copy.114) | copy-start | bytes 73732
  572.5 23.6 %copy-start.20 = (f32[1,3,8,256]{3,1,2,0:T(4,128)}, f32[1,3,8,256]{3,1,2,0:T(4,128)S(1)}, u32[]{:S(2)}) copy-start(f32[1,3,8,256]{3,1,2,0:T(4,128)S(1)} %copy.112) | copy-start | bytes 73732
  572.6 26.4 %copy-start.17 = (f32[1,3,8,256]{3,1,2,0:T(4,128)}, f32[1,3,8,256]{3,1,2,0:T(4,128)S(1)}, u32[]{:S(2)}) copy-start(f32[1,3,8,256]{3,1,2,0:T(4,128)S(1)} %copy.116) | copy-start | bytes 73732
  578.2 2.6 copy-start.25
  580.6 6.8 copy-start.22
  582.7 9.1 all-to-all-start.1
  587.4 193.2 %all-gather.15.cloned.1.call-start = ((), (), s32[]{:S(2)}) async-start(), calls=%async_computation.7 | async-start | bytes 1597440 | tf_op jit(solution)/shard_map/all_gather | solution.py:31
  592.9 0.7 copy-start.26
  593.2 2.9 copy-start.24
  593.3 2.9 copy-start.11
  593.3 2.2 copy-start.7
  593.3 2.8 copy-start.5
  593.4 2.1 copy-start.9
  600.2 3.7 copy-start.1
  602.0 0.8 copy-start.2
  640.8 13.1 %copy-start.21 = (f32[1,3,8,256]{3,1,2,0:T(4,128)S(1)}, f32[1,3,8,256]{3,1,2,0:T(4,128)}, u32[]{:S(2)}) copy-start(f32[1,3,8,256]{3,1,2,0:T(4,128)} %copy-done.20) | copy-start | bytes 73732
  640.8 13.6 %copy-start.16 = (f32[1,3,8,256]{3,1,2,0:T(4,128)S(1)}, f32[1,3,8,256]{3,1,2,0:T(4,128)}, u32[]{:S(2)}) copy-start(f32[1,3,8,256]{3,1,2,0:T(4,128)} %copy-done.15) | copy-start | bytes 73732
  640.8 14.7 %copy-start.12 = (f32[1,6,8,256]{3,1,2,0:T(8,128)S(1)}, f32[1,6,8,256]{3,1,2,0:T(8,128)}, u32[]{:S(2)}) copy-start(f32[1,6,8,256]{3,1,2,0:T(8,128)} %copy-done.11) | copy-start | bytes 147460
  642.1 2.8 collective-permute-start.2
  643.4 5.7 collective-permute-start.3
  652.2 428.6 %all-gather.11.cloned.1.call-start = ((), (), s32[]{:S(2)}) async-start(), calls=%async_computation.5 | async-start | bytes 1597440 | tf_op jit(solution)/shard_map/all_gather | solution.py:31
  652.5 2.4 copy-start.18
  652.5 3.0 copy-start.3
  653.9 132.4 %copy-start.8 = (f32[1,6,8,256]{3,1,2,0:T(8,128)S(1)}, f32[1,6,8,256]{3,1,2,0:T(8,128)}, u32[]{:S(2)}) copy-start(f32[1,6,8,256]{3,1,2,0:T(8,128)} %copy-done.7) | copy-start | bytes 147460
  654.4 132.3 %copy-start.10 = (f32[1,6,8,256]{3,1,2,0:T(8,128)S(1)}, f32[1,6,8,256]{3,1,2,0:T(8,128)}, u32[]{:S(2)}) copy-start(f32[1,6,8,256]{3,1,2,0:T(8,128)} %copy-done.9) | copy-start | bytes 147460
  655.0 132.3 %copy-start.6 = (f32[1,6,8,256]{3,1,2,0:T(8,128)S(1)}, f32[1,6,8,256]{3,1,2,0:T(8,128)}, u32[]{:S(2)}) copy-start(f32[1,6,8,256]{3,1,2,0:T(8,128)} %copy-done.5) | copy-start | bytes 147460
  787.3 267.1 %copy-start.4 = (f32[3,4,8,256]{3,2,1,0:T(8,128)S(1)}, f32[3,4,8,256]{3,2,1,0:T(8,128)}, u32[]{:S(2)}) copy-start(f32[3,4,8,256]{3,2,1,0:T(8,128)} %param.19) | copy-start | bytes 294916
  787.3 293.6 %copy-start.28 = (f32[64,1,1]{0,2,1:T(1,128)S(1)}, f32[64,1,1]{0,2,1:T(1,128)}, u32[]{:S(2)}) copy-start(f32[64,1,1]{0,2,1:T(1,128)} %copy-done.27) | copy-start | bytes 772
  1053.2 154.2 %copy-start.23 = (f32[3,8,256]{2,1,0:T(8,128)S(1)}, f32[3,8,256]{2,1,0:T(8,128)}, u32[]{:S(2)}) copy-start(f32[3,8,256]{2,1,0:T(8,128)} %get-tuple-element.325) | copy-start | bytes 73732
  1053.2 156.0 %copy-start.14 = (f32[3,4,8,256]{3,2,1,0:T(8,128)S(1)}, f32[3,4,8,256]{3,2,1,0:T(8,128)}, u32[]{:S(2)}) copy-start(f32[3,4,8,256]{3,2,1,0:T(8,128)} %param.20) | copy-start | bytes 294916
Sparse Core Ops, SparseCore 0:
  20.4 146.7 all-gather.12
  185.0 252.5 all-gather.8
  652.4 128.1 all-gather.14
  785.7 295.1 all-gather.10
where the time goes:
time: 1230 us; the launch traced here: 1220 us
  blocking collectives  428 us (35%)
  waiting for transfers between devices  418 us (34%)
  other arithmetic  201 us (16%)
  local copies, waits for them, and re-layouts  110 us (9%)
  matrix products  20.8 us (2%)
  between operations  20.8 us (2%)
  starting transfers between devices  17.2 us (1%)
    all_gather x4, waiting for transfers between devices, carried_in(): gathered = jax.tree.map(lambda a: lax.all_gather(a, axis), part)  403 us
    psum x1, blocking collectives, local(): totals = lax.psum((sum_in, sum_bias, sum_out), ('gx', 'gy'))  262 us
    add x126, other arithmetic, combine(): return (earlier[0] * later[0], later[0] * earlier[1] + later[1])  174 us
    unnamed x1, blocking collectives  149 us
    dynamic_slice x126, local copies, waits for them, and re-layouts, one(): lax.dynamic_index_in_dim(a, source, 0, False)  77 us
  transfers between devices with their start and end apart: 10, of which 8 were waited for; matrix products, arithmetic and copies ran while one was open for 1% of the time, Pallas kernels for 0%

commit v1 on v0

v1 whole, which is shorter than its diff:
```python
import functools

import jax
import jax.numpy as jnp
import ml_dtypes
import numpy as np
from jax import lax
from jax.experimental import pallas as pl
from jax.experimental.pallas import tpu as pltpu
from jax.sharding import PartitionSpec as P

FILTER_ALPHA = 0.499
FILTER_GAIN = 0.5 + FILTER_ALPHA
COMPACT_ALPHA = 1.0 / 3.0
STEP_SIZE = 0.5
MESH = pl.DeviceIdType.MESH
F32 = jnp.float32
BF16 = jnp.bfloat16

GROUP = 4
RING = 16
LINE = 8
ROWS = 4
UNITS = 64

UP_W, DOWN_W, UP_C, DOWN_C, RING_L, RING_R, BACK_L, BACK_R, LOCAL, LEFT, RIGHT = (
    0, 4, 8, 12, 16, 32, 48, 68, 88, 104, 108
)


def tridiagonal(length, coupling):
    return np.eye(length) + coupling * (np.eye(length, k=1) + np.eye(length, k=-1))


def smoothing_table():
    devices = GROUP * RING
    length = devices * ROWS
    matrix = tridiagonal(length, FILTER_ALPHA)
    inverse = np.linalg.inv(matrix)
    smoothing = np.linalg.solve(matrix, FILTER_GAIN * tridiagonal(length, 0.5))

    def move(row, pivot):
        return inverse[row, pivot] / inverse[pivot, pivot]

    table = np.zeros((devices, 128))
    block = GROUP * ROWS
    for device in range(devices):
        ring, member = divmod(device, GROUP)
        first = device * ROWS
        last = first + ROWS - 1
        entry = table[device]
        if device < devices - 1:
            entry[UP_W:UP_W + ROWS] = smoothing[last + 1, first:first + ROWS]
        if device > 0:
            entry[DOWN_W:DOWN_W + ROWS] = smoothing[first - 1, first:first + ROWS]
        group_first = ring * block
        group_last = group_first + block - 1
        for other in range(GROUP):
            start = group_first + other * ROWS
            if ring < RING - 1:
                entry[UP_C + other] = move(group_last + 1, start + ROWS)
            if ring > 0:
                entry[DOWN_C + other] = move(group_first - 1, start - 1)
        for other in range(RING):
            if other < ring:
                entry[RING_L + other] = move(group_first, (other + 1) * block)
            if other > ring:
                entry[RING_R + other] = move(group_last, other * block - 1)
        for target in range(GROUP):
            own_first = group_first + target * ROWS
            own_last = own_first + ROWS - 1
            entry[BACK_L + 5 * target] = move(own_first, group_first)
            entry[BACK_R + 5 * target] = move(own_last, group_last)
            for other in range(GROUP):
                start = group_first + other * ROWS
                if other < target:
                    entry[BACK_L + 5 * target + 1 + other] = move(own_first, start + ROWS)
                if other > target:
                    entry[BACK_R + 5 * target + 1 + other] = move(own_last, start - 1)
        entry[LOCAL:LOCAL + ROWS * ROWS] = smoothing[first:last + 1, first:last + 1].reshape(-1)
        for row in range(ROWS):
            entry[LEFT + row] = move(first + row, first)
            entry[RIGHT + row] = move(first + row, last)
    return table.astype(np.float32)


def derivative_matrix(length):
    right = 7.0 / 9.0 * (np.eye(length, k=1) - np.eye(length, k=-1)) + 1.0 / 36.0 * (
        np.eye(length, k=2) - np.eye(length, k=-2)
    )
    return np.linalg.solve(tridiagonal(length, COMPACT_ALPHA), right)


def line_table():
    size = 8
    length = LINE * size
    forward = derivative_matrix(length)
    table = np.zeros((LINE, size, 128))
    for place, matrix in enumerate((forward, forward.T)):
        base = 24 * place
        for device in range(LINE):
            rows = slice(device * size, device * size + size)
            table[device, :, base:base + 8] = matrix[rows, rows]
            if device < LINE - 1:
                table[device, 0, base + 8:base + 16] = matrix[device * size + 8, rows]
                table[device, 1, base + 8:base + 16] = matrix[device * size + 9, rows]
            if device > 0:
                table[device, 2, base + 8:base + 16] = matrix[device * size - 1, rows]
                table[device, 3, base + 8:base + 16] = matrix[device * size - 2, rows]
            for source in range(LINE):
                if source == device:
                    continue
                columns = slice(source * size, source * size + size)
                pivot = source * size + 9 if source < device else source * size - 2
                sent = matrix[pivot, columns]
                factors = matrix[rows, columns] @ sent / (sent @ sent)
                if source == device - 1:
                    factors[0] = 0.0
                if source == device + 1:
                    factors[size - 1] = 0.0
                table[device, :, base + 16 + source] = factors
    table[1:, 0, 48] = 1.0
    table[:-1, size - 1, 49] = 1.0
    return table.astype(np.float32)


def split_table(matrix):
    high = matrix.astype(np.float32).astype(ml_dtypes.bfloat16)
    low = (matrix - high.astype(np.float64)).astype(np.float32).astype(ml_dtypes.bfloat16)
    return [high, low]


def depth_table(length):
    matrix = derivative_matrix(length)
    return np.stack(split_table(matrix.T.copy()) + split_table(matrix))


def split(values):
    high = values.astype(BF16)
    return high, (values - high.astype(F32)).astype(BF16)


def iota(shape, dim):
    return lax.broadcasted_iota(jnp.int32, shape, dim)


def ones_where(condition):
    return jnp.where(condition, 1.0, 0.0).astype(F32)


def matmul(a, b):
    return jnp.dot(a, b, preferred_element_type=F32)


def matmul_nt(a, b, precision=None):
    return lax.dot_general(a, b, (((1,), (1,)), ((), ())), precision=precision, preferred_element_type=F32)


def kernel(
    velocity, cotangent, weight_in, bias_in, weight_out, x_table, y_table, z_table,
    new_velocity, grad_velocity, grad_in, grad_bias, grad_out_t,
    vel, cot, smoothed, feats, gfeats, pulled, nvel, gvel, scalars, columns, tall, ztab,
    left_lhs, back_lhs, force_lhs, rhs, pre_buf, sums,
    x1_send, x1_recv, x2_send, x2_recv, x3_send, x3_recv, y_send, y_recv, y_edge,
    p1, p2, p3,
    local_sem, x1_ss, x1_rs, x2_ss, x2_rs, x3_ss, x3_rs, y_ss, y_rs, ye_ss, ye_rs,
    p1_ss, p1_rs, p2_ss, p2_rs, p3_ss, p3_rs,
):
    gx = lax.axis_index("gx")
    gy = lax.axis_index("gy")
    ring = lax.div(gx, GROUP)
    member = lax.rem(gx, GROUP)

    def in_group(step):
        return lax.rem(member + step, GROUP)

    def in_ring(step):
        return lax.rem(ring + step, RING)

    def in_line(step):
        return lax.rem(gy + step, LINE)

    def group_device(other):
        return (ring * GROUP + other, gy)

    def ring_device(other):
        return (other * GROUP + member, gy)

    def line_device(other):
        return (gx, other)

    barrier = pltpu.get_barrier_semaphore()
    partners = (
        [ring_device(in_ring(step)) for step in range(1, RING)]
        + [group_device(in_group(step)) for step in range(1, GROUP)]
        + [line_device(in_line(step)) for step in range(1, LINE)]
    )
    for partner in partners:
        pl.semaphore_signal(barrier, inc=1, device_id=partner, device_id_type=MESH)

    loads = [
        pltpu.make_async_copy(velocity, vel, local_sem.at[0]),
        pltpu.make_async_copy(x_table.at[gx], scalars, local_sem.at[1]),
        pltpu.make_async_copy(y_table.at[gy], columns, local_sem.at[2]),
        pltpu.make_async_copy(cotangent, cot, local_sem.at[3]),
        pltpu.make_async_copy(z_table, ztab, local_sem.at[4]),
    ]
    for load in loads:
        load.start()

    def remote(src, dst, send_sem, recv_sem, device):
        return pltpu.make_async_remote_copy(
            src_ref=src, dst_ref=dst, send_sem=send_sem, recv_sem=recv_sem, device_id=device, device_id_type=MESH
        )

    sent = []

    def send(*args):
        copy = remote(*args)
        copy.start()
        sent.append(copy)

    def scalar(index):
        return scalars[0, index]

    def build_weights():
        w_high, w_low = split(weight_in[...])
        spread = ones_where(lax.shift_right_logical(iota((512, UNITS), 0), 3) == iota((512, UNITS), 1)).astype(BF16)
        spread_t = ones_where(iota((UNITS, 512), 0) == lax.shift_right_logical(iota((UNITS, 512), 1), 3)).astype(BF16)
        bias = bias_in[...]
        b_high, b_low = split(bias)
        b_rest = bias - b_high.astype(F32) - b_low.astype(F32)
        row = iota((8, 256), 0)
        col = iota((8, 256), 1)
        field = lax.shift_right_logical(col, 3)
        pick_high = ones_where(((field == row) | (field == row + 6)) & (row < 6)).astype(BF16)
        pick_low = ones_where((field == row + 12) & (row < 6)).astype(BF16)
        spread_high = matmul_nt(spread, w_high).astype(BF16)
        spread_low = matmul_nt(spread, w_low).astype(BF16)
        top = matmul(spread_high, pick_high[0:6]) + matmul(spread_low, pick_low[0:6])
        same = lax.bitwise_and(iota((512, 256), 0), 7) == lax.bitwise_and(iota((512, 256), 1), 7)
        top = jnp.where(same, top, 0.0)
        biases = jnp.concatenate([b_high.astype(F32), b_low.astype(F32), b_rest, jnp.zeros((5, UNITS), F32)], axis=0)
        spread_bias = matmul_nt(spread, biases.astype(BF16)).astype(BF16)
        top = top + matmul(spread_bias, ones_where(col == row + 240).astype(BF16))
        left_lhs[0:512, :] = top.astype(BF16)
        o_high, o_low = split(weight_out[...])
        pick_high = ones_where(((field == row + 18) | (field == row + 22)) & (row < 3)).astype(BF16)
        pick_low = ones_where((field == row + 26) & (row < 3)).astype(BF16)
        spread_oh = matmul(spread, o_high).astype(BF16)
        spread_ol = matmul(spread, o_low).astype(BF16)
        bottom = matmul(spread_oh, pick_high[0:3]) + matmul(spread_ol, pick_low[0:3])
        left_lhs[512:1024, :] = jnp.where(same, bottom, 0.0).astype(BF16)

        same_t = lax.bitwise_and(iota((96, 512), 0), 7) == lax.bitwise_and(iota((96, 512), 1), 7)
        row = lax.shift_right_logical(iota((96, 8), 0), 3)
        col = iota((96, 8), 1)
        get_high = ones_where((row == col) & (col < 6)).astype(BF16)
        get_low = ones_where((row == col + 6) & (col < 6)).astype(BF16)
        tall_w = matmul(get_high[:, 0:6], w_high) + matmul(get_low[:, 0:6], w_low)
        back_lhs[...] = jnp.where(same_t, matmul(tall_w.astype(BF16), spread_t), 0.0).astype(BF16)
        get_high = ones_where((row[0:64] == col[0:64]) & (col[0:64] < 3)).astype(BF16)
        get_low = ones_where((row[0:64] == col[0:64] + 4) & (col[0:64] < 3)).astype(BF16)
        tall_o = matmul_nt(get_high[:, 0:3], o_high) + matmul_nt(get_low[:, 0:3], o_low)
        force_lhs[...] = jnp.where(same_t[0:64], matmul(tall_o.astype(BF16), spread_t), 0.0).astype(BF16)

    build_weights()
    loads[0].wait()
    loads[1].wait()
    loads[2].wait()
    line_columns = columns[...]
    for index in range(50):
        tall[index] = jnp.broadcast_to(line_columns[:, index:index + 1], (8, 128))

    def tall_column(index):
        half = tall[index]
        return jnp.concatenate([half, half], axis=1)

    def smooth(src, order, after_barrier, meanwhile, emit):
        for comp in range(3):
            rows = [src[comp, row] for row in range(ROWS)]
            for kind, base in ((0, UP_W), (1, DOWN_W)):
                state = sum(scalar(base + row) * rows[row] for row in range(ROWS))
                for piece in range(GROUP):
                    x1_send[order, piece, kind, comp] = state[2 * piece:2 * piece + 2]
        after_barrier()
        for step in (2, 1, 3):
            other = in_group(step)
            send(
                x1_send.at[order, other], x1_recv.at[order, member],
                x1_ss.at[order, other], x1_rs.at[order, member], group_device(other),
            )
        x1_recv[order, member] = x1_send[order, member]
        meanwhile()
        for step in range(1, GROUP):
            other = in_group(step)
            remote(
                x1_send.at[order, other], x1_recv.at[order, other],
                x1_ss.at[order, other], x1_rs.at[order, other], group_device(other),
            ).wait_recv()
        ups = [x1_recv[order, other, 0] for other in range(GROUP)]
        downs = [x1_recv[order, other, 1] for other in range(GROUP)]
        x2_send[order, 0] = sum(scalar(UP_C + other) * ups[other] for other in range(GROUP))
        x2_send[order, 1] = sum(scalar(DOWN_C + other) * downs[other] for other in range(GROUP))
        for step in (8, 7, 9, 6, 10, 5, 11, 4, 12, 3, 13, 2, 14, 1, 15):
            other = in_ring(step)
            kind = jnp.where(other > ring, 0, 1)
            send(
                x2_send.at[order, kind], x2_recv.at[order, ring],
                x2_ss.at[order, other], x2_rs.at[order, ring], ring_device(other),
            )
        left = jnp.zeros((3, 2, 256), F32)
        right = jnp.zeros((3, 2, 256), F32)
        for step in (1, 15, 2, 14, 3, 13, 4, 12, 5, 11, 6, 10, 7, 9, 8):
            other = in_ring(step)
            remote(
                x2_send.at[order, 0], x2_recv.at[order, other],
                x2_ss.at[order, other], x2_rs.at[order, other], ring_device(other),
            ).wait_recv()
            part = x2_recv[order, other]
            left = left + scalar(RING_L + other) * part
            right = right + scalar(RING_R + other) * part
        for step in (2, 1, 3, 0):
            other = in_group(step)
            target_left = scalar(BACK_L + 5 * other) * left
            target_right = scalar(BACK_R + 5 * other) * right
            for source in range(GROUP):
                target_left = target_left + scalar(BACK_L + 5 * other + 1 + source) * ups[source]
                target_right = target_right + scalar(BACK_R + 5 * other + 1 + source) * downs[source]
            if step == 0:
                x3_recv[order, member, 0] = target_left
                x3_recv[order, member, 1] = target_right
            else:
                x3_send[order, other, 0] = target_left
                x3_send[order, other, 1] = target_right
                send(
                    x3_send.at[order, other], x3_recv.at[order, member],
                    x3_ss.at[order, other], x3_rs.at[order, member], group_device(other),
                )
        for step in range(1, GROUP):
            other = in_group(step)
            remote(
                x3_send.at[order, other], x3_recv.at[order, other],
                x3_ss.at[order, other], x3_rs.at[order, other], group_device(other),
            ).wait_recv()
        for comp in range(3):
            rows = [src[comp, row] for row in range(ROWS)]
            from_left = jnp.concatenate([x3_recv[order, piece, 0, comp] for piece in range(GROUP)], axis=0)
            from_right = jnp.concatenate([x3_recv[order, piece, 1, comp] for piece in range(GROUP)], axis=0)
            for row in range(ROWS):
                total = scalar(LEFT + row) * from_left + scalar(RIGHT + row) * from_right
                for col in range(ROWS):
                    total = total + scalar(LOCAL + ROWS * row + col) * rows[col]
                emit(comp, row, total)

    def line_send(load, order):
        base = 24 * order
        sent_columns = [tall_column(base + 8 + col) for col in range(8)]
        for comp in range(3):
            for row in range(ROWS):
                tile = load(comp, row)
                out = sum(sent_columns[col] * tile[col:col + 1] for col in range(8))
                for kind in range(4):
                    y_send[order, kind, comp, row:row + 1, :] = out[kind:kind + 1]
        for kind, step in ((0, 1), (1, LINE - 1)):
            send(
                y_send.at[order, 2 * kind], y_edge.at[order, kind],
                ye_ss.at[order, kind], ye_rs.at[order, kind], line_device(in_line(step)),
            )
        for step in (4, 5, 3, 2, 6, 1, 7):
            other = in_line(step)
            kind = jnp.where(other > gy, 1, 3)
            send(
                y_send.at[order, kind], y_recv.at[order, gy],
                y_ss.at[order, other], y_rs.at[order, gy], line_device(other),
            )

    def line_local(load, order, store):
        base = 24 * order
        local_columns = [tall_column(base + col) for col in range(8)]
        for comp in range(3):
            for row in range(ROWS):
                tile = load(comp, row)
                store(comp, row, sum(local_columns[col] * tile[col:col + 1] for col in range(8)))

    def line_receive(order, load, store):
        base = 24 * order
        for kind, step in ((0, LINE - 1), (1, 1)):
            remote(
                y_send.at[order, 0], y_edge.at[order, kind],
                ye_ss.at[order, kind], ye_rs.at[order, kind], line_device(in_line(step)),
            ).wait_recv()
        for step in range(1, LINE):
            other = in_line(step)
            remote(
                y_send.at[order, 1], y_recv.at[order, other],
                y_ss.at[order, other], y_rs.at[order, other], line_device(other),
            ).wait_recv()
        y_recv[order, gy] = jnp.zeros((3, ROWS, 256), F32)
        factors = [tall_column(base + 16 + source) for source in range(LINE)]
        first = tall_column(48)
        last = tall_column(49)
        for comp in range(3):
            for row in range(ROWS):
                total = load(comp, row)
                total = total + first * y_edge[order, 0, comp, row:row + 1, :]
                total = total + last * y_edge[order, 1, comp, row:row + 1, :]
                for source in range(LINE):
                    total = total + factors[source] * y_recv[order, source, comp, row:row + 1, :]
                store(comp, row, total)

    def depth_apply(values, order):
        high, low = split(values)
        both = matmul(jnp.concatenate([high, low], axis=0), ztab[2 * order])
        count = values.shape[0]
        return both[0:count] + both[count:2 * count] + matmul(high, ztab[2 * order + 1])

    def wait_barrier():
        pl.semaphore_wait(barrier, len(partners))

    def nothing():
        pass

    def keep_smoothed(comp, row, value):
        smoothed[comp, row] = value

    def load_waits():
        loads[3].wait()
        loads[4].wait()

    smooth(vel, 0, wait_barrier, load_waits, keep_smoothed)

    line_send(lambda comp, row: smoothed[comp, row], 0)
    along_z = depth_apply(smoothed[...].reshape(96, 256), 0)
    for comp in range(3):
        for row in range(ROWS):
            start = (comp * ROWS + row) * 8
            feats[row, 24 + 8 * comp:32 + 8 * comp, :] = along_z[start:start + 8]

    def store_feature(comp, row, value):
        feats[row, 8 * comp:8 * comp + 8, :] = value

    line_local(lambda comp, row: smoothed[comp, row], 0, store_feature)
    line_receive(0, lambda comp, row: feats[row, 8 * comp:8 * comp + 8, :], store_feature)

    def outward(row):
        parts = [STEP_SIZE * cot[comp, row] for comp in range(3)]
        return jnp.concatenate(parts + [jnp.zeros((8, 256), F32)], axis=0)

    def closure(row, carry):
        feature_high, feature_low = split(feats[row])
        rhs[0:48, :] = feature_high
        rhs[48:96, :] = feature_low
        rhs[96:144, :] = feature_high
        out_high, out_low = split(outward(row))
        rhs[144:176, :] = out_high
        rhs[176:208, :] = out_low
        rhs[208:240, :] = out_high
        rhs[240:256, :] = jnp.ones((16, 256), BF16)
        hidden = jnp.tanh(matmul(left_lhs[0:512, :], rhs[...]))
        grad_pre = matmul(left_lhs[512:1024, :], rhs[...]) * (1.0 - hidden * hidden)
        pre_buf[row, 0] = hidden
        pre_buf[row, 1] = grad_pre
        pre_high, pre_low = split(grad_pre)
        both = matmul(back_lhs[...], pre_high)
        gfeats[row] = both[0:48] + both[48:96] + matmul(back_lhs[0:48, :], pre_low)
        return carry

    lax.fori_loop(0, ROWS, closure, 0)

    line_send(lambda comp, row: gfeats[row, 8 * comp:8 * comp + 8, :], 1)
    back_in = jnp.concatenate(
        [gfeats[row, 24 + 8 * comp:32 + 8 * comp, :] for comp in range(3) for row in range(ROWS)], axis=0
    )
    along_z = depth_apply(back_in, 1)

    def add_depth(comp, row, value):
        start = (comp * ROWS + row) * 8
        pulled[comp, row] = value + along_z[start:start + 8]

    line_local(lambda comp, row: gfeats[row, 8 * comp:8 * comp + 8, :], 1, add_depth)

    def forces_and_sums(row, carry):
        hidden = pre_buf[row, 0]
        hidden_high, hidden_low = split(hidden)
        both = matmul(force_lhs[...], hidden_high)
        forcing = both[0:32] + both[32:64] + matmul(force_lhs[0:32, :], hidden_low)
        for comp in range(3):
            nvel[comp, row] = vel[comp, row] + STEP_SIZE * forcing[8 * comp:8 * comp + 8]
        with_ones = jnp.concatenate([feats[row], jnp.ones((8, 256), F32)], axis=0)
        sums[0:56, :] += matmul_nt(with_ones, pre_buf[row, 1], lax.Precision.HIGHEST)
        sums[56:88, :] += matmul_nt(outward(row), hidden, lax.Precision.HIGHEST)
        return carry

    def partial_sums():
        sums[...] = jnp.zeros((88, 512), F32)
        lax.fori_loop(0, ROWS, forces_and_sums, 0)
        same = lax.bitwise_and(iota((88, 512), 0), 7) == lax.bitwise_and(iota((88, 512), 1), 7)
        gather = ones_where(lax.shift_right_logical(iota((512, UNITS), 0), 3) == iota((512, UNITS), 1))
        fold = ones_where(iota((16, 88), 0) == lax.shift_right_logical(iota((16, 88), 1), 3))
        narrow = jnp.dot(
            jnp.where(same, sums[...], 0.0), gather, precision=lax.Precision.HIGHEST, preferred_element_type=F32
        )
        p1[gy] = jnp.dot(fold, narrow, precision=lax.Precision.HIGHEST, preferred_element_type=F32)
        for step in range(1, LINE):
            other = in_line(step)
            send(p1.at[gy], p1.at[gy], p1_ss.at[other], p1_rs.at[gy], line_device(other))

    line_receive(1, lambda comp, row: pulled[comp, row], lambda comp, row, value: pulled.__setitem__((comp, row), value))

    def keep_gradient(comp, row, value):
        gvel[comp, row] = cot[comp, row] + value

    smooth(pulled, 1, nothing, partial_sums, keep_gradient)

    stores = [
        pltpu.make_async_copy(nvel, new_velocity, local_sem.at[0]),
        pltpu.make_async_copy(gvel, grad_velocity, local_sem.at[1]),
    ]
    for store in stores:
        store.start()

    for step in range(1, LINE):
        other = in_line(step)
        remote(p1.at[other], p1.at[other], p1_ss.at[other], p1_rs.at[other], line_device(other)).wait_recv()
    total = p1[0]
    for other in range(1, LINE):
        total = total + p1[other]
    p2[member] = total
    for step in range(1, GROUP):
        other = in_group(step)
        send(p2.at[member], p2.at[member], p2_ss.at[other], p2_rs.at[member], group_device(other))
    for step in range(1, GROUP):
        other = in_group(step)
        remote(p2.at[other], p2.at[other], p2_ss.at[other], p2_rs.at[other], group_device(other)).wait_recv()
    total = p2[0]
    for other in range(1, GROUP):
        total = total + p2[other]
    p3[ring] = total
    for step in range(1, RING):
        other = in_ring(step)
        send(p3.at[ring], p3.at[ring], p3_ss.at[other], p3_rs.at[ring], ring_device(other))
    for step in range(1, RING):
        other = in_ring(step)
        remote(p3.at[other], p3.at[other], p3_ss.at[other], p3_rs.at[other], ring_device(other)).wait_recv()
    total = p3[0]
    for other in range(1, RING):
        total = total + p3[other]
    total = total * (1.0 / float(256 * 64 * 256))
    grad_in[...] = total[0:6]
    grad_bias[...] = total[6:7]
    grad_out_t[...] = total[7:10]

    for copy in sent:
        copy.wait_send()
    for store in stores:
        store.wait()


def local(velocity, cotangent, weight_in, bias_in, weight_out):
    field = velocity.shape
    dma = pltpu.SemaphoreType.DMA
    anywhere = pl.BlockSpec(memory_space=pl.ANY)
    whole = pl.BlockSpec(memory_space=pltpu.VMEM)
    outs = pl.pallas_call(
        kernel,
        out_shape=(
            jax.ShapeDtypeStruct(field, F32),
            jax.ShapeDtypeStruct(field, F32),
            jax.ShapeDtypeStruct((6, UNITS), F32),
            jax.ShapeDtypeStruct((1, UNITS), F32),
            jax.ShapeDtypeStruct((3, UNITS), F32),
        ),
        in_specs=[anywhere, anywhere, whole, whole, whole, anywhere, anywhere, anywhere],
        out_specs=(anywhere, anywhere, whole, whole, whole),
        scratch_shapes=[
            pltpu.VMEM(field, F32),
            pltpu.VMEM(field, F32),
            pltpu.VMEM(field, F32),
            pltpu.VMEM((ROWS, 48, 256), F32),
            pltpu.VMEM((ROWS, 48, 256), F32),
            pltpu.VMEM(field, F32),
            pltpu.VMEM(field, F32),
            pltpu.VMEM(field, F32),
            pltpu.SMEM((1, 128), F32),
            pltpu.VMEM((8, 128), F32),
            pltpu.VMEM((50, 8, 128), F32),
            pltpu.VMEM((4, 256, 256), BF16),
            pltpu.VMEM((1024, 256), BF16),
            pltpu.VMEM((96, 512), BF16),
            pltpu.VMEM((64, 512), BF16),
            pltpu.VMEM((256, 256), BF16),
            pltpu.VMEM((ROWS, 2, 512, 256), F32),
            pltpu.VMEM((88, 512), F32),
            pltpu.VMEM((2, GROUP, 2, 3, 2, 256), F32),
            pltpu.VMEM((2, GROUP, 2, 3, 2, 256), F32),
            pltpu.VMEM((2, 2, 3, 2, 256), F32),
            pltpu.VMEM((2, RING, 3, 2, 256), F32),
            pltpu.VMEM((2, GROUP, 2, 3, 2, 256), F32),
            pltpu.VMEM((2, GROUP, 2, 3, 2, 256), F32),
            pltpu.VMEM((2, 4, 3, ROWS, 256), F32),
            pltpu.VMEM((2, LINE, 3, ROWS, 256), F32),
            pltpu.VMEM((2, 2, 3, ROWS, 256), F32),
            pltpu.VMEM((LINE, 16, UNITS), F32),
            pltpu.VMEM((GROUP, 16, UNITS), F32),
            pltpu.VMEM((RING, 16, UNITS), F32),
            dma((5,)),
            dma((2, GROUP)), dma((2, GROUP)),
            dma((2, RING)), dma((2, RING)),
            dma((2, GROUP)), dma((2, GROUP)),
            dma((2, LINE)), dma((2, LINE)),
            dma((2, 2)), dma((2, 2)),
            dma((LINE,)), dma((LINE,)),
            dma((GROUP,)), dma((GROUP,)),
            dma((RING,)), dma((RING,)),
        ],
        compiler_params=pltpu.CompilerParams(collective_id=0, has_side_effects=True),
        name="closure_step",
    )(
        velocity, cotangent, weight_in, bias_in.reshape(1, UNITS), weight_out,
        jnp.asarray(smoothing_table()).reshape(GROUP * RING, 1, 128), jnp.asarray(line_table()),
        jnp.asarray(depth_table(field[3])),
    )
    return outs[0], outs[1], outs[2], outs[3].reshape(UNITS), outs[4].T


def solution(mesh):
    in_specs = (P(None, "gx", "gy", None), P(None, "gx", "gy", None), P(), P(), P())
    out_specs = (P(None, "gx", "gy", None), P(None, "gx", "gy", None), P(), P(), P())
    return jax.shard_map(local, mesh=mesh, in_specs=in_specs, out_specs=out_specs, check_vma=False)
```

time: 1230 us -> 77.5 us (0.06)
  the two profiles are of different devices: /device:TPU:2 before, /device:TPU:8 now
where the time goes in v1:
time: 77.5 us; the launch traced here: 77.2 us
  Pallas kernels  71.2 us (92%)
  local copies, waits for them, and re-layouts  5.41 us (7%)
    pallas_call x1, Pallas kernels, local(): pl.pallas_call(kernel, out_shape=(jax.ShapeDtypeStruct(field, F32), jax.S...  71.2 us
    unnamed x14, local copies, waits for them, and re-layouts  5.41 us

profile of v1, /device:TPU:8, one launch (start us, length us, event | category | flops | bytes accessed | tf_op | source)
XLA Modules:
  0.0 77.2 jit_solution(1513008470326910484)
XLA Ops:
  0.6 1.4 %copy.13.weight_out = f32[64,3]{1,0:T(8,128)} copy(f32[64,3]{0,1:T(4,128)} %param.12) | data formatting | bytes 1536 | tf_op args[4]
  2.0 71.2 %closure_step.1 = (f32[3,4,8,256]{3,2,1,0:T(8,128)}, f32[3,4,8,256]{3,2,1,0:T(8,128)}, f32[6,64]{1,0:T(8,128)}, f32[1,64]{1,0:T(1,128)}, f32[3,64]{1,0:T(4,128)}) custom-call(f32[3,4,8,256]{3,2,1,0:T(8,128)} %velocity.1, f32[3,4,8,256]{3,2,1,0:T(8,128)} %cotangent.1, f32[6,64]{1,0:T(8,128)} %weight_in.1, f32[1,64]{1,0:T(1,128)} %bitcast.4, ...), custom_call_target="tpu_custom_call" | custom-call | tf_op jit(solution)/shard_map/closure_step/pallas_call | solution.py:565
  73.2 0.0 copy-start
  73.2 1.6 %copy.19 = f32[3,4,8,256]{3,2,1,0:T(8,128)} copy(f32[3,4,8,256]{3,2,1,0:T(8,128)} %get-tuple-element.20) | data formatting | bytes 196608
  74.8 0.0 copy-done
  74.8 0.0 copy-start.1
  74.8 0.6 copy.20
  75.4 0.0 copy-done.1
  75.5 0.0 copy-start.3
  75.5 0.0 copy-start.2
  75.5 0.6 copy.21
  76.1 0.1 copy-done.3
  76.1 0.5 copy.22
  76.7 0.0 copy-done.2
  76.7 0.6 copy.23
Async XLA Ops:
  73.2 1.6 %copy-start = (f32[3,4,8,256]{3,2,1,0:T(8,128)S(1)}, f32[3,4,8,256]{3,2,1,0:T(8,128)}, u32[]{:S(2)}) copy-start(f32[3,4,8,256]{3,2,1,0:T(8,128)} %get-tuple-element.21) | copy-start | bytes 294916
  74.8 0.7 copy-start.1
  75.5 0.7 copy-start.3
  75.5 1.2 %copy-start.2 = (f32[3,64]{1,0:T(4,128)S(1)}, f32[3,64]{1,0:T(4,128)}, u32[]{:S(2)}) copy-start(f32[3,64]{1,0:T(4,128)} %get-tuple-element.14) | copy-start | bytes 2308

commit v2 on v1

--- a/solution.py
+++ b/solution.py
@@ -158,12 +158,12 @@
 
 def kernel(
     velocity, cotangent, weight_in, bias_in, weight_out, x_table, y_table, z_table,
-    new_velocity, grad_velocity, grad_in, grad_bias, grad_out_t,
-    vel, cot, smoothed, feats, gfeats, pulled, nvel, gvel, scalars, columns, tall, ztab,
-    left_lhs, back_lhs, force_lhs, rhs, pre_buf, sums,
+    new_velocity, grad_velocity, grad_weights,
+    w_in, w_bias, w_out, vel, cot, smoothed, feats, gfeats, pulled, nvel, gvel, scalars, columns, tall, ztab,
+    left_lhs, back_lhs, force_lhs, rhs, hidden_buf, pre_buf, sums, totals,
     x1_send, x1_recv, x2_send, x2_recv, x3_send, x3_recv, y_send, y_recv, y_edge,
     p1, p2, p3,
-    local_sem, x1_ss, x1_rs, x2_ss, x2_rs, x3_ss, x3_rs, y_ss, y_rs, ye_ss, ye_rs,
+    token, local_sem, x1_ss, x1_rs, x2_ss, x2_rs, x3_ss, x3_rs, y_ss, y_rs, ye_ss, ye_rs,
     p1_ss, p1_rs, p2_ss, p2_rs, p3_ss, p3_rs,
 ):
     gx = lax.axis_index("gx")
@@ -190,8 +190,10 @@
         return (gx, other)
 
     barrier = pltpu.get_barrier_semaphore()
+    half = RING // 4
+    near = list(range(1, half + 1)) + list(range(RING - half, RING))
     partners = (
-        [ring_device(in_ring(step)) for step in range(1, RING)]
+        [ring_device(in_ring(step)) for step in near]
         + [group_device(in_group(step)) for step in range(1, GROUP)]
         + [line_device(in_line(step)) for step in range(1, LINE)]
     )
@@ -199,11 +201,14 @@
         pl.semaphore_signal(barrier, inc=1, device_id=partner, device_id_type=MESH)
 
     loads = [
-        pltpu.make_async_copy(velocity, vel, local_sem.at[0]),
-        pltpu.make_async_copy(x_table.at[gx], scalars, local_sem.at[1]),
+        pltpu.make_async_copy(x_table.at[gx], scalars, local_sem.at[0]),
+        pltpu.make_async_copy(velocity, vel, local_sem.at[1]),
         pltpu.make_async_copy(y_table.at[gy], columns, local_sem.at[2]),
-        pltpu.make_async_copy(cotangent, cot, local_sem.at[3]),
-        pltpu.make_async_copy(z_table, ztab, local_sem.at[4]),
+        pltpu.make_async_copy(weight_in, w_in, local_sem.at[3]),
+        pltpu.make_async_copy(bias_in, w_bias, local_sem.at[4]),
+        pltpu.make_async_copy(weight_out, w_out, local_sem.at[5]),
+        pltpu.make_async_copy(cotangent, cot, local_sem.at[6]),
+        pltpu.make_async_copy(z_table, ztab, local_sem.at[7]),
     ]
     for load in loads:
         load.start()
@@ -224,10 +229,10 @@
         return scalars[0, index]
 
     def build_weights():
-        w_high, w_low = split(weight_in[...])
+        w_high, w_low = split(w_in[...])
         spread = ones_where(lax.shift_right_logical(iota((512, UNITS), 0), 3) == iota((512, UNITS), 1)).astype(BF16)
         spread_t = ones_where(iota((UNITS, 512), 0) == lax.shift_right_logical(iota((UNITS, 512), 1), 3)).astype(BF16)
-        bias = bias_in[...]
+        bias = w_bias[...]
         b_high, b_low = split(bias)
         b_rest = bias - b_high.astype(F32) - b_low.astype(F32)
         row = iota((8, 256), 0)
@@ -244,11 +249,11 @@
         spread_bias = matmul_nt(spread, biases.astype(BF16)).astype(BF16)
         top = top + matmul(spread_bias, ones_where(col == row + 240).astype(BF16))
         left_lhs[0:512, :] = top.astype(BF16)
-        o_high, o_low = split(weight_out[...])
+        o_high, o_low = split(w_out[...])
         pick_high = ones_where(((field == row + 18) | (field == row + 22)) & (row < 3)).astype(BF16)
         pick_low = ones_where((field == row + 26) & (row < 3)).astype(BF16)
-        spread_oh = matmul(spread, o_high).astype(BF16)
-        spread_ol = matmul(spread, o_low).astype(BF16)
+        spread_oh = matmul_nt(spread, o_high).astype(BF16)
+        spread_ol = matmul_nt(spread, o_low).astype(BF16)
         bottom = matmul(spread_oh, pick_high[0:3]) + matmul(spread_ol, pick_low[0:3])
         left_lhs[512:1024, :] = jnp.where(same, bottom, 0.0).astype(BF16)
 
@@ -261,29 +266,30 @@
         back_lhs[...] = jnp.where(same_t, matmul(tall_w.astype(BF16), spread_t), 0.0).astype(BF16)
         get_high = ones_where((row[0:64] == col[0:64]) & (col[0:64] < 3)).astype(BF16)
         get_low = ones_where((row[0:64] == col[0:64] + 4) & (col[0:64] < 3)).astype(BF16)
-        tall_o = matmul_nt(get_high[:, 0:3], o_high) + matmul_nt(get_low[:, 0:3], o_low)
+        tall_o = matmul(get_high[:, 0:3], o_high) + matmul(get_low[:, 0:3], o_low)
         force_lhs[...] = jnp.where(same_t[0:64], matmul(tall_o.astype(BF16), spread_t), 0.0).astype(BF16)
 
-    build_weights()
-    loads[0].wait()
-    loads[1].wait()
-    loads[2].wait()
-    line_columns = columns[...]
-    for index in range(50):
-        tall[index] = jnp.broadcast_to(line_columns[:, index:index + 1], (8, 128))
+    def build_columns():
+        loads[2].wait()
+        line_columns = columns[...]
+        for index in range(50):
+            tall[index] = jnp.broadcast_to(line_columns[:, index:index + 1], (8, 128))
+        for load in loads[3:6]:
+            load.wait()
+        build_weights()
 
     def tall_column(index):
         half = tall[index]
         return jnp.concatenate([half, half], axis=1)
 
-    def smooth(src, order, after_barrier, meanwhile, emit):
+    def smooth(src, order, before_send, in_first, before_second, in_second, late_second, emit):
         for comp in range(3):
             rows = [src[comp, row] for row in range(ROWS)]
             for kind, base in ((0, UP_W), (1, DOWN_W)):
                 state = sum(scalar(base + row) * rows[row] for row in range(ROWS))
                 for piece in range(GROUP):
                     x1_send[order, piece, kind, comp] = state[2 * piece:2 * piece + 2]
-        after_barrier()
+        before_send()
         for step in (2, 1, 3):
             other = in_group(step)
             send(
@@ -291,7 +297,7 @@
                 x1_ss.at[order, other], x1_rs.at[order, member], group_device(other),
             )
         x1_recv[order, member] = x1_send[order, member]
-        meanwhile()
+        in_first()
         for step in range(1, GROUP):
             other = in_group(step)
             remote(
@@ -302,6 +308,7 @@
         downs = [x1_recv[order, other, 1] for other in range(GROUP)]
         x2_send[order, 0] = sum(scalar(UP_C + other) * ups[other] for other in range(GROUP))
         x2_send[order, 1] = sum(scalar(DOWN_C + other) * downs[other] for other in range(GROUP))
+        before_second()
         for step in (8, 7, 9, 6, 10, 5, 11, 4, 12, 3, 13, 2, 14, 1, 15):
             other = in_ring(step)
             kind = jnp.where(other > ring, 0, 1)
@@ -309,9 +316,12 @@
                 x2_send.at[order, kind], x2_recv.at[order, ring],
                 x2_ss.at[order, other], x2_rs.at[order, ring], ring_device(other),
             )
+        in_second()
         left = jnp.zeros((3, 2, 256), F32)
         right = jnp.zeros((3, 2, 256), F32)
         for step in (1, 15, 2, 14, 3, 13, 4, 12, 5, 11, 6, 10, 7, 9, 8):
+            if step == 5:
+                late_second()
             other = in_ring(step)
             remote(
                 x2_send.at[order, 0], x2_recv.at[order, other],
@@ -415,8 +425,16 @@
         count = values.shape[0]
         return both[0:count] + both[count:2 * count] + matmul(high, ztab[2 * order + 1])
 
-    def wait_barrier():
+    def pass_tokens():
         pl.semaphore_wait(barrier, len(partners))
+        for kind, step in ((0, half), (1, RING - half)):
+            pl.semaphore_signal(
+                token.at[kind], inc=1, device_id=ring_device(in_ring(step)), device_id_type=MESH
+            )
+
+    def wait_tokens():
+        for kind in range(2):
+            pl.semaphore_wait(token.at[kind], 1)
 
     def nothing():
         pass
@@ -424,11 +442,14 @@
     def keep_smoothed(comp, row, value):
         smoothed[comp, row] = value
 
-    def load_waits():
-        loads[3].wait()
-        loads[4].wait()
-
-    smooth(vel, 0, wait_barrier, load_waits, keep_smoothed)
+    def load_rest():
+        for load in loads[6:]:
+            load.wait()
+
+    loads[0].wait()
+    loads[1].wait()
+    build_columns()
+    smooth(vel, 0, pass_tokens, load_rest, wait_tokens, nothing, nothing, keep_smoothed)
 
     line_send(lambda comp, row: smoothed[comp, row], 0)
     along_z = depth_apply(smoothed[...].reshape(96, 256), 0)
@@ -459,9 +480,10 @@
         rhs[240:256, :] = jnp.ones((16, 256), BF16)
         hidden = jnp.tanh(matmul(left_lhs[0:512, :], rhs[...]))
         grad_pre = matmul(left_lhs[512:1024, :], rhs[...]) * (1.0 - hidden * hidden)
-        pre_buf[row, 0] = hidden
-        pre_buf[row, 1] = grad_pre
         pre_high, pre_low = split(grad_pre)
+        hidden_buf[row] = hidden
+        pre_buf[row, 0] = pre_high
+        pre_buf[row, 1] = pre_low
         both = matmul(back_lhs[...], pre_high)
         gfeats[row] = both[0:48] + both[48:96] + matmul(back_lhs[0:48, :], pre_low)
         return carry
@@ -481,80 +503,112 @@
     line_local(lambda comp, row: gfeats[row, 8 * comp:8 * comp + 8, :], 1, add_depth)
 
     def forces_and_sums(row, carry):
-        hidden = pre_buf[row, 0]
-        hidden_high, hidden_low = split(hidden)
+        hidden_high, hidden_low = split(hidden_buf[row])
         both = matmul(force_lhs[...], hidden_high)
         forcing = both[0:32] + both[32:64] + matmul(force_lhs[0:32, :], hidden_low)
         for comp in range(3):
             nvel[comp, row] = vel[comp, row] + STEP_SIZE * forcing[8 * comp:8 * comp + 8]
-        with_ones = jnp.concatenate([feats[row], jnp.ones((8, 256), F32)], axis=0)
-        sums[0:56, :] += matmul_nt(with_ones, pre_buf[row, 1], lax.Precision.HIGHEST)
-        sums[56:88, :] += matmul_nt(outward(row), hidden, lax.Precision.HIGHEST)
+        feature_high, feature_low = split(feats[row])
+        ones = jnp.ones((16, 256), BF16)
+        both = matmul_nt(jnp.concatenate([feature_high, ones, feature_low], axis=0), pre_buf[row, 0])
+        rest = matmul_nt(jnp.concatenate([feature_high, ones], axis=0), pre_buf[row, 1])
+        sums[0:48, :] += both[0:48] + both[64:112] + rest[0:48]
+        sums[48:56, :] += both[48:56] + rest[48:56]
+        out_high, out_low = split(outward(row))
+        both = matmul_nt(jnp.concatenate([out_high, out_low], axis=0), hidden_high)
+        rest = matmul_nt(out_high, hidden_low)
+        sums[56:88, :] += both[0:32] + both[32:64] + rest
         return carry
 
-    def partial_sums():
+    def first_sums():
         sums[...] = jnp.zeros((88, 512), F32)
-        lax.fori_loop(0, ROWS, forces_and_sums, 0)
+        lax.fori_loop(0, ROWS // 2, forces_and_sums, 0)
+
+    def last_sums():
+        lax.fori_loop(ROWS // 2, ROWS, forces_and_sums, 0)
         same = lax.bitwise_and(iota((88, 512), 0), 7) == lax.bitwise_and(iota((88, 512), 1), 7)
-        gather = ones_where(lax.shift_right_logical(iota((512, UNITS), 0), 3) == iota((512, UNITS), 1))
-        fold = ones_where(iota((16, 88), 0) == lax.shift_right_logical(iota((16, 88), 1), 3))
-        narrow = jnp.dot(
-            jnp.where(same, sums[...], 0.0), gather, precision=lax.Precision.HIGHEST, preferred_element_type=F32
-        )
-        p1[gy] = jnp.dot(fold, narrow, precision=lax.Precision.HIGHEST, preferred_element_type=F32)
+        gather = ones_where(lax.shift_right_logical(iota((512, UNITS), 0), 3) == iota((512, UNITS), 1)).astype(BF16)
+        high, low = split(jnp.where(same, sums[...], 0.0))
+        narrow = matmul(high, gather) + matmul(low, gather)
+        folded = [jnp.sum(narrow[8 * part:8 * part + 8], axis=0, keepdims=True) for part in range(11)]
+        front = jnp.concatenate(folded[0:8], axis=0)
+        back = jnp.concatenate(folded[8:11] + [jnp.zeros((5, UNITS), F32)], axis=0)
+        p1[gy] = jnp.concatenate([front, back], axis=1)
         for step in range(1, LINE):
             other = in_line(step)
             send(p1.at[gy], p1.at[gy], p1_ss.at[other], p1_rs.at[gy], line_device(other))
 
-    line_receive(1, lambda comp, row: pulled[comp, row], lambda comp, row, value: pulled.__setitem__((comp, row), value))
+    def sum_line():
+        for step in range(1, LINE):
+            other = in_line(step)
+            remote(p1.at[other], p1.at[other], p1_ss.at[other], p1_rs.at[other], line_device(other)).wait_recv()
+        total = p1[0]
+        for other in range(1, LINE):
+            total = total + p1[other]
+        p2[member] = total
+        for step in range(1, GROUP):
+            other = in_group(step)
+            send(p2.at[member], p2.at[member], p2_ss.at[other], p2_rs.at[member], group_device(other))
+
+    def sum_group():
+        for step in range(1, GROUP):
+            other = in_group(step)
+            remote(p2.at[other], p2.at[other], p2_ss.at[other], p2_rs.at[other], group_device(other)).wait_recv()
+        total = p2[0]
+        for other in range(1, GROUP):
+            total = total + p2[other]
+        p3[ring] = total
+        for step in (8, 7, 9, 6, 10, 5, 11, 4, 12, 3, 13, 2, 14, 1, 15):
+            other = in_ring(step)
+            send(p3.at[ring], p3.at[ring], p3_ss.at[other], p3_rs.at[ring], ring_device(other))
+
+    def sum_ring():
+        for step in range(1, RING):
+            other = in_ring(step)
+            remote(p3.at[other], p3.at[other], p3_ss.at[other], p3_rs.at[other], ring_device(other)).wait_recv()
+        total = p3[0]
+        for other in range(1, RING):
+            total = total + p3[other]
+        totals[...] = total * (1.0 / float(256 * 64 * 256))
+
+    first_sums()
+
+    def keep_pulled(comp, row, value):
+        pulled[comp, row] = value
+
+    line_receive(1, lambda comp, row: pulled[comp, row], keep_pulled)
 
     def keep_gradient(comp, row, value):
         gvel[comp, row] = cot[comp, row] + value
-
-    smooth(pulled, 1, nothing, partial_sums, keep_gradient)
 
     stores = [
         pltpu.make_async_copy(nvel, new_velocity, local_sem.at[0]),
         pltpu.make_async_copy(gvel, grad_velocity, local_sem.at[1]),
+        pltpu.make_async_copy(totals, grad_weights, local_sem.at[2]),
     ]
-    for store in stores:
-        store.start()
-
-    for step in range(1, LINE):
-        other = in_line(step)
-        remote(p1.at[other], p1.at[other], p1_ss.at[other], p1_rs.at[other], line_device(other)).wait_recv()
-    total = p1[0]
-    for other in range(1, LINE):
-        total = total + p1[other]
-    p2[member] = total
-    for step in range(1, GROUP):
-        other = in_group(step)
-        send(p2.at[member], p2.at[member], p2_ss.at[other], p2_rs.at[member], group_device(other))
-    for step in range(1, GROUP):
-        other = in_group(step)
-        remote(p2.at[other], p2.at[other], p2_ss.at[other], p2_rs.at[other], group_device(other)).wait_recv()
-    total = p2[0]
-    for other in range(1, GROUP):
-        total = total + p2[other]
-    p3[ring] = total
-    for step in range(1, RING):
-        other = in_ring(step)
-        send(p3.at[ring], p3.at[ring], p3_ss.at[other], p3_rs.at[ring], ring_device(other))
-    for step in range(1, RING):
-        other = in_ring(step)
-        remote(p3.at[other], p3.at[other], p3_ss.at[other], p3_rs.at[other], ring_device(other)).wait_recv()
-    total = p3[0]
-    for other in range(1, RING):
-        total = total + p3[other]
-    total = total * (1.0 / float(256 * 64 * 256))
-    grad_in[...] = total[0:6]
-    grad_bias[...] = total[6:7]
-    grad_out_t[...] = total[7:10]
-
+
+    def store_velocity():
+        stores[0].start()
+        sum_line()
+
+    smooth(pulled, 1, nothing, last_sums, nothing, store_velocity, sum_group, keep_gradient)
+    stores[1].start()
+    sum_ring()
+    stores[2].start()
     for copy in sent:
         copy.wait_send()
     for store in stores:
         store.wait()
+
+
+def finish(new_velocity_in, grad_velocity_in, grads, new_velocity, grad_velocity, grad_in, grad_bias, grad_out_t):
+    new_velocity[...] = new_velocity_in[...]
+    grad_velocity[...] = grad_velocity_in[...]
+    front = grads[:, 0:UNITS]
+    grad_in[...] = front[0:6]
+    grad_bias[...] = front[6:7]
+    grad_out_t[0:1] = front[7:8]
+    grad_out_t[1:3] = grads[0:2, UNITS:2 * UNITS]
 
 
 def local(velocity, cotangent, weight_in, bias_in, weight_out):
@@ -562,18 +616,19 @@
     dma = pltpu.SemaphoreType.DMA
     anywhere = pl.BlockSpec(memory_space=pl.ANY)
     whole = pl.BlockSpec(memory_space=pltpu.VMEM)
-    outs = pl.pallas_call(
+    mid = pl.pallas_call(
         kernel,
         out_shape=(
             jax.ShapeDtypeStruct(field, F32),
             jax.ShapeDtypeStruct(field, F32),
-            jax.ShapeDtypeStruct((6, UNITS), F32),
-            jax.ShapeDtypeStruct((1, UNITS), F32),
-            jax.ShapeDtypeStruct((3, UNITS), F32),
+            jax.ShapeDtypeStruct((8, 128), F32),
         ),
-        in_specs=[anywhere, anywhere, whole, whole, whole, anywhere, anywhere, anywhere],
-        out_specs=(anywhere, anywhere, whole, whole, whole),
+        in_specs=[anywhere] * 8,
+        out_specs=(anywhere, anywhere, anywhere),
         scratch_shapes=[
+            pltpu.VMEM((6, UNITS), F32),
+            pltpu.VMEM((1, UNITS), F32),
+            pltpu.VMEM((3, UNITS), F32),
             pltpu.VMEM(field, F32),
             pltpu.VMEM(field, F32),
             pltpu.VMEM(field, F32),
@@ -590,8 +645,10 @@
             pltpu.VMEM((96, 512), BF16),
             pltpu.VMEM((64, 512), BF16),
             pltpu.VMEM((256, 256), BF16),
-            pltpu.VMEM((ROWS, 2, 512, 256), F32),
+            pltpu.VMEM((ROWS, 512, 256), F32),
+            pltpu.VMEM((ROWS, 2, 512, 256), BF16),
             pltpu.VMEM((88, 512), F32),
+            pltpu.VMEM((8, 128), F32),
             pltpu.VMEM((2, GROUP, 2, 3, 2, 256), F32),
             pltpu.VMEM((2, GROUP, 2, 3, 2, 256), F32),
             pltpu.VMEM((2, 2, 3, 2, 256), F32),
@@ -601,10 +658,11 @@
             pltpu.VMEM((2, 4, 3, ROWS, 256), F32),
             pltpu.VMEM((2, LINE, 3, ROWS, 256), F32),
             pltpu.VMEM((2, 2, 3, ROWS, 256), F32),
-            pltpu.VMEM((LINE, 16, UNITS), F32),
-            pltpu.VMEM((GROUP, 16, UNITS), F32),
-            pltpu.VMEM((RING, 16, UNITS), F32),
-            dma((5,)),
+            pltpu.VMEM((LINE, 8, 128), F32),
+            pltpu.VMEM((GROUP, 8, 128), F32),
+            pltpu.VMEM((RING, 8, 128), F32),
+            pltpu.SemaphoreType.REGULAR((2,)),
+            dma((8,)),
             dma((2, GROUP)), dma((2, GROUP)),
             dma((2, RING)), dma((2, RING)),
             dma((2, GROUP)), dma((2, GROUP)),
@@ -617,10 +675,23 @@
         compiler_params=pltpu.CompilerParams(collective_id=0, has_side_effects=True),
         name="closure_step",
     )(
-        velocity, cotangent, weight_in, bias_in.reshape(1, UNITS), weight_out,
+        velocity, cotangent, weight_in, bias_in.reshape(1, UNITS), weight_out.T,
         jnp.asarray(smoothing_table()).reshape(GROUP * RING, 1, 128), jnp.asarray(line_table()),
         jnp.asarray(depth_table(field[3])),
     )
+    outs = pl.pallas_call(
+        finish,
+        out_shape=(
+            jax.ShapeDtypeStruct(field, F32),
+            jax.ShapeDtypeStruct(field, F32),
+            jax.ShapeDtypeStruct((6, UNITS), F32),
+            jax.ShapeDtypeStruct((1, UNITS), F32),
+            jax.ShapeDtypeStruct((3, UNITS), F32),
+        ),
+        in_specs=[whole] * 3,
+        out_specs=(whole,) * 5,
+        name="finish",
+    )(*mid)
     return outs[0], outs[1], outs[2], outs[3].reshape(UNITS), outs[4].T
 
 

time: 77.5 us -> 59.1 us (0.76)
  the two profiles are of different devices: /device:TPU:8 before, /device:TPU:2 now
where the time goes in v2:
time: 59.1 us; the launch traced here: 58.9 us
  Pallas kernels  58.3 us (99%)
  between operations  0.64 us (1%)
    pallas_call x1, Pallas kernels, local(): pl.pallas_call(kernel, out_shape=(jax.ShapeDtypeStruct(field, F32), jax.S...  56.6 us
    pallas_call x1, Pallas kernels, local(): pl.pallas_call(finish, out_shape=(jax.ShapeDtypeStruct(field, F32), jax.S...  1.64 us

profile of v2, /device:TPU:2, one launch (start us, length us, event | category | flops | bytes accessed | tf_op | source)
XLA Modules:
  0.0 58.9 jit_solution(8304909522693384627)
XLA Ops:
  0.6 56.6 %closure_step.1 = (f32[3,4,8,256]{3,2,1,0:T(8,128)}, f32[3,4,8,256]{3,2,1,0:T(8,128)}, f32[8,128]{1,0:T(8,128)}) custom-call(f32[3,4,8,256]{3,2,1,0:T(8,128)} %velocity.1, f32[3,4,8,256]{3,2,1,0:T(8,128)} %cotangent.1, f32[6,64]{1,0:T(8,128)} %weight_in.1, f32[1,64]{1,0:T(1,128)} %bitcast.5, f32[3,64]{1,0:T(4,128)} %bitcast.4, ...), custom_call_target="tpu_custom_call" | custom-call | tf_op jit(solution)/shard_map/closure_step/pallas_call | solution.py:619
  57.3 1.6 %finish.1 = (f32[3,4,8,256]{3,2,1,0:T(8,128)}, f32[3,4,8,256]{3,2,1,0:T(8,128)}, f32[6,64]{1,0:T(8,128)}, f32[1,64]{1,0:T(1,128)}, f32[3,64]{1,0:T(4,128)}) custom-call(f32[3,4,8,256]{3,2,1,0:T(8,128)} %get-tuple-element.13.new_velocity_in, f32[3,4,8,256]{3,2,1,0:T(8,128)} %get-tuple-element.14.grad_velocity_in, f32[8,128]{1,0:T(8,128)} %get-tuple-element.15.grads), custom_call_target="tpu_custom_call" | custom-call | tf_op jit(solution)/shard_map/finish/pallas_call | solution.py:682

commit v3 on v2

--- a/solution.py
+++ b/solution.py
@@ -107,9 +107,8 @@
             if device > 0:
                 table[device, 2, base + 8:base + 16] = matrix[device * size - 1, rows]
                 table[device, 3, base + 8:base + 16] = matrix[device * size - 2, rows]
-            for source in range(LINE):
-                if source == device:
-                    continue
+            for step in range(1, LINE):
+                source = (device - step) % LINE
                 columns = slice(source * size, source * size + size)
                 pivot = source * size + 9 if source < device else source * size - 2
                 sent = matrix[pivot, columns]
@@ -118,7 +117,7 @@
                     factors[0] = 0.0
                 if source == device + 1:
                     factors[size - 1] = 0.0
-                table[device, :, base + 16 + source] = factors
+                table[device, :, base + 16 + step] = factors
     table[1:, 0, 48] = 1.0
     table[:-1, size - 1, 49] = 1.0
     return table.astype(np.float32)
@@ -159,11 +158,14 @@
 def kernel(
     velocity, cotangent, weight_in, bias_in, weight_out, x_table, y_table, z_table,
     new_velocity, grad_velocity, grad_weights,
-    w_in, w_bias, w_out, vel, cot, smoothed, feats, gfeats, pulled, nvel, gvel, scalars, columns, tall, ztab,
+    w_in, w_bias, w_out, vel, cot, along_y, smoothed, feats, gfeats, pulled, nvel, gvel,
+    scalars, columns, tall, ztab,
     left_lhs, back_lhs, force_lhs, rhs, hidden_buf, pre_buf, sums, totals,
-    x1_send, x1_recv, x2_send, x2_recv, x3_send, x3_recv, y_send, y_recv, y_edge,
+    x1_send, x1_recv, state, x2_send, x2_recv, x3_send, x3_recv, plane_send, plane_recv, plane_edge,
+    y_send, y_recv, y_edge,
     p1, p2, p3,
-    token, local_sem, x1_ss, x1_rs, x2_ss, x2_rs, x3_ss, x3_rs, y_ss, y_rs, ye_ss, ye_rs,
+    token, local_sem, x1_ss, x1_rs, x2_ss, x2_rs, x3_ss, x3_rs, plane_ss, plane_rs, edge_ss, edge_rs,
+    y_ss, y_rs, ye_ss, ye_rs,
     p1_ss, p1_rs, p2_ss, p2_rs, p3_ss, p3_rs,
 ):
     gx = lax.axis_index("gx")
@@ -189,13 +191,18 @@
     def line_device(other):
         return (gx, other)
 
+    def plane_device(other, place):
+        return (ring * GROUP + other, place)
+
     barrier = pltpu.get_barrier_semaphore()
     half = RING // 4
     near = list(range(1, half + 1)) + list(range(RING - half, RING))
     partners = (
         [ring_device(in_ring(step)) for step in near]
-        + [group_device(in_group(step)) for step in range(1, GROUP)]
-        + [line_device(in_line(step)) for step in range(1, LINE)]
+        + [
+            plane_device(in_group(step), in_line(along))
+            for step in range(GROUP) for along in range(LINE) if step or along
+        ]
     )
     for partner in partners:
         pl.semaphore_signal(barrier, inc=1, device_id=partner, device_id_type=MESH)
@@ -220,15 +227,18 @@
 
     sent = []
 
-    def send(*args):
+    def send(*args, drain=True):
         copy = remote(*args)
         copy.start()
-        sent.append(copy)
+        if drain:
+            sent.append(copy)
 
     def scalar(index):
         return scalars[0, index]
 
     def build_weights():
+        for load in loads[3:6]:
+            load.wait()
         w_high, w_low = split(w_in[...])
         spread = ones_where(lax.shift_right_logical(iota((512, UNITS), 0), 3) == iota((512, UNITS), 1)).astype(BF16)
         spread_t = ones_where(iota((UNITS, 512), 0) == lax.shift_right_logical(iota((UNITS, 512), 1), 3)).astype(BF16)
@@ -274,41 +284,70 @@
         line_columns = columns[...]
         for index in range(50):
             tall[index] = jnp.broadcast_to(line_columns[:, index:index + 1], (8, 128))
-        for load in loads[3:6]:
-            load.wait()
-        build_weights()
 
     def tall_column(index):
         half = tall[index]
         return jnp.concatenate([half, half], axis=1)
 
-    def smooth(src, order, before_send, in_first, before_second, in_second, late_second, emit):
-        for comp in range(3):
-            rows = [src[comp, row] for row in range(ROWS)]
-            for kind, base in ((0, UP_W), (1, DOWN_W)):
-                state = sum(scalar(base + row) * rows[row] for row in range(ROWS))
-                for piece in range(GROUP):
-                    x1_send[order, piece, kind, comp] = state[2 * piece:2 * piece + 2]
-        before_send()
+    lower = iota((8, 128), 1) < 64
+
+    def turn(tile):
+        return pltpu.roll(tile, 64, 1)
+
+    def pack(left, right, piece):
+        lanes = slice(128 * (piece // 2), 128 * (piece // 2) + 128)
+        if piece % 2 == 0:
+            return jnp.where(lower, left[:, lanes], turn(right[:, lanes]))
+        return jnp.where(lower, turn(left[:, lanes]), right[:, lanes])
+
+    def unpack(pieces):
+        left = [jnp.where(lower, pieces[2 * t], turn(pieces[2 * t + 1])) for t in range(2)]
+        right = [jnp.where(lower, turn(pieces[2 * t]), pieces[2 * t + 1]) for t in range(2)]
+        return jnp.concatenate(left, axis=1), jnp.concatenate(right, axis=1)
+
+    def two_scalars(left_index, right_index):
+        return jnp.where(lower, scalar(left_index), scalar(right_index))
+
+    def states(rows):
+        return [sum(scalar(base + row) * rows[row] for row in range(ROWS)) for base in (UP_W, DOWN_W)]
+
+    def local_rows(rows):
+        return [
+            sum(scalar(LOCAL + ROWS * row + col) * rows[col] for col in range(ROWS)) for row in range(ROWS)
+        ]
+
+    def pieces_send(source, target, send_sems, recv_sems, order):
         for step in (2, 1, 3):
             other = in_group(step)
             send(
-                x1_send.at[order, other], x1_recv.at[order, member],
-                x1_ss.at[order, other], x1_rs.at[order, member], group_device(other),
+                source.at[order, other], target.at[order, member],
+                send_sems.at[order, other], recv_sems.at[order, member], group_device(other),
             )
-        x1_recv[order, member] = x1_send[order, member]
-        in_first()
+
+    def pieces_wait(source, target, send_sems, recv_sems, order):
         for step in range(1, GROUP):
             other = in_group(step)
             remote(
-                x1_send.at[order, other], x1_recv.at[order, other],
-                x1_ss.at[order, other], x1_rs.at[order, other], group_device(other),
+                source.at[order, other], target.at[order, other],
+                send_sems.at[order, other], recv_sems.at[order, other], group_device(other),
             ).wait_recv()
-        ups = [x1_recv[order, other, 0] for other in range(GROUP)]
-        downs = [x1_recv[order, other, 1] for other in range(GROUP)]
-        x2_send[order, 0] = sum(scalar(UP_C + other) * ups[other] for other in range(GROUP))
-        x2_send[order, 1] = sum(scalar(DOWN_C + other) * downs[other] for other in range(GROUP))
-        before_second()
+
+    def ring_send(order, load):
+        gathered = []
+        for comp in range(3):
+            gathered.append(sum(
+                two_scalars(UP_C + other, DOWN_C + other) * load(other, comp) for other in range(GROUP)
+            ))
+        first, second, third = gathered
+        turned = turn(third)
+        front = jnp.where(lower, first, turn(second))
+        x2_send[order, 0, 0] = front[0:4]
+        x2_send[order, 0, 1] = front[4:8]
+        x2_send[order, 0, 2] = jnp.where(lower[0:4], third[0:4], turned[4:8])
+        front = jnp.where(lower, turn(first), second)
+        x2_send[order, 1, 0] = front[0:4]
+        x2_send[order, 1, 1] = front[4:8]
+        x2_send[order, 1, 2] = jnp.where(lower[0:4], turned[0:4], third[4:8])
         for step in (8, 7, 9, 6, 10, 5, 11, 4, 12, 3, 13, 2, 14, 1, 15):
             other = in_ring(step)
             kind = jnp.where(other > ring, 0, 1)
@@ -316,12 +355,13 @@
                 x2_send.at[order, kind], x2_recv.at[order, ring],
                 x2_ss.at[order, other], x2_rs.at[order, ring], ring_device(other),
             )
-        in_second()
-        left = jnp.zeros((3, 2, 256), F32)
-        right = jnp.zeros((3, 2, 256), F32)
+
+    def ring_receive(order, midway):
+        left = jnp.zeros((3, 4, 128), F32)
+        right = jnp.zeros((3, 4, 128), F32)
         for step in (1, 15, 2, 14, 3, 13, 4, 12, 5, 11, 6, 10, 7, 9, 8):
             if step == 5:
-                late_second()
+                midway()
             other = in_ring(step)
             remote(
                 x2_send.at[order, 0], x2_recv.at[order, other],
@@ -330,38 +370,68 @@
             part = x2_recv[order, other]
             left = left + scalar(RING_L + other) * part
             right = right + scalar(RING_R + other) * part
+        front_left = jnp.concatenate([left[0], left[1]], axis=0)
+        front_right = jnp.concatenate([right[0], right[1]], axis=0)
+        back_left = jnp.concatenate([left[2], pltpu.roll(left[2], 64, 1)], axis=0)
+        back_right = jnp.concatenate([pltpu.roll(right[2], 64, 1), right[2]], axis=0)
+        return [
+            jnp.where(lower, front_left, turn(front_right)),
+            jnp.where(lower, turn(front_left), front_right),
+            jnp.where(lower, back_left, back_right),
+        ]
+
+    def back_piece(ring_state, load, other, comp):
+        total = two_scalars(BACK_L + 5 * other, BACK_R + 5 * other) * ring_state[comp]
+        for source in range(GROUP):
+            index = 5 * other + 1 + source
+            total = total + two_scalars(BACK_L + index, BACK_R + index) * load(source, comp)
+        return total
+
+    def project(order, other, comp, tile):
+        out = sum(tall[24 * order + 8 + col] * tile[col:col + 1] for col in range(8))
+        for kind in range(4):
+            plane_send[order, other, kind, comp:comp + 1, :] = out[kind:kind + 1]
+
+    def plane_rows_send(order):
         for step in (2, 1, 3, 0):
             other = in_group(step)
-            target_left = scalar(BACK_L + 5 * other) * left
-            target_right = scalar(BACK_R + 5 * other) * right
-            for source in range(GROUP):
-                target_left = target_left + scalar(BACK_L + 5 * other + 1 + source) * ups[source]
-                target_right = target_right + scalar(BACK_R + 5 * other + 1 + source) * downs[source]
-            if step == 0:
-                x3_recv[order, member, 0] = target_left
-                x3_recv[order, member, 1] = target_right
-            else:
-                x3_send[order, other, 0] = target_left
-                x3_send[order, other, 1] = target_right
+            for along in (4, 5, 3, 6, 2, 7, 1):
+                place = in_line(along)
+                kind = jnp.where(place > gy, 1, 3)
                 send(
-                    x3_send.at[order, other], x3_recv.at[order, member],
-                    x3_ss.at[order, other], x3_rs.at[order, member], group_device(other),
+                    plane_send.at[order, other, kind], plane_recv.at[order, member, along - 1],
+                    plane_ss.at[order], plane_rs.at[order], plane_device(other, place), drain=False,
                 )
-        for step in range(1, GROUP):
-            other = in_group(step)
-            remote(
-                x3_send.at[order, other], x3_recv.at[order, other],
-                x3_ss.at[order, other], x3_rs.at[order, other], group_device(other),
-            ).wait_recv()
-        for comp in range(3):
-            rows = [src[comp, row] for row in range(ROWS)]
-            from_left = jnp.concatenate([x3_recv[order, piece, 0, comp] for piece in range(GROUP)], axis=0)
-            from_right = jnp.concatenate([x3_recv[order, piece, 1, comp] for piece in range(GROUP)], axis=0)
-            for row in range(ROWS):
-                total = scalar(LEFT + row) * from_left + scalar(RIGHT + row) * from_right
-                for col in range(ROWS):
-                    total = total + scalar(LOCAL + ROWS * row + col) * rows[col]
-                emit(comp, row, total)
+            for kind, along in ((0, 1), (1, LINE - 1)):
+                send(
+                    plane_send.at[order, other, 2 * kind], plane_edge.at[order, member, kind],
+                    edge_ss.at[order], edge_rs.at[order], plane_device(other, in_line(along)), drain=False,
+                )
+
+    def plane_rows_all(order):
+        device = plane_device(in_group(1), in_line(1))
+        return (
+            remote(plane_recv.at[order], plane_recv.at[order], plane_ss.at[order], plane_rs.at[order], device),
+            remote(plane_edge.at[order], plane_edge.at[order], edge_ss.at[order], edge_rs.at[order], device),
+        )
+
+    def plane_rows_wait(order):
+        for copy in plane_rows_all(order):
+            copy.wait_recv()
+
+    def plane_rows_drain(order):
+        for copy in plane_rows_all(order):
+            copy.wait_send()
+
+    def from_plane(order, source, comp):
+        total = tall[48] * plane_edge[order, source, 0, comp:comp + 1, :]
+        total = total + tall[49] * plane_edge[order, source, 1, comp:comp + 1, :]
+        for along in range(1, LINE):
+            total = total + tall[24 * order + 16 + along] * plane_recv[order, source, along - 1, comp:comp + 1, :]
+        return total
+
+    def own_block(order, tile):
+        return sum(tall[24 * order + col] * tile[col:col + 1] for col in range(8))
 
     def line_send(load, order):
         base = 24 * order
@@ -381,8 +451,8 @@
             other = in_line(step)
             kind = jnp.where(other > gy, 1, 3)
             send(
-                y_send.at[order, kind], y_recv.at[order, gy],
-                y_ss.at[order, other], y_rs.at[order, gy], line_device(other),
+                y_send.at[order, kind], y_recv.at[order, step - 1],
+                y_ss.at[order, step - 1], y_rs.at[order, step - 1], line_device(other),
             )
 
     def line_local(load, order, store):
@@ -401,13 +471,11 @@
                 ye_ss.at[order, kind], ye_rs.at[order, kind], line_device(in_line(step)),
             ).wait_recv()
         for step in range(1, LINE):
-            other = in_line(step)
             remote(
-                y_send.at[order, 1], y_recv.at[order, other],
-                y_ss.at[order, other], y_rs.at[order, other], line_device(other),
+                y_send.at[order, 1], y_recv.at[order, step - 1],
+                y_ss.at[order, step - 1], y_rs.at[order, step - 1], line_device(in_line(step)),
             ).wait_recv()
-        y_recv[order, gy] = jnp.zeros((3, ROWS, 256), F32)
-        factors = [tall_column(base + 16 + source) for source in range(LINE)]
+        factors = [tall_column(base + 16 + step) for step in range(1, LINE)]
         first = tall_column(48)
         last = tall_column(49)
         for comp in range(3):
@@ -415,8 +483,8 @@
                 total = load(comp, row)
                 total = total + first * y_edge[order, 0, comp, row:row + 1, :]
                 total = total + last * y_edge[order, 1, comp, row:row + 1, :]
-                for source in range(LINE):
-                    total = total + factors[source] * y_recv[order, source, comp, row:row + 1, :]
+                for step in range(1, LINE):
+                    total = total + factors[step - 1] * y_recv[order, step - 1, comp, row:row + 1, :]
                 store(comp, row, total)
 
     def depth_apply(values, order):
@@ -439,30 +507,65 @@
     def nothing():
         pass
 
-    def keep_smoothed(comp, row, value):
-        smoothed[comp, row] = value
-
-    def load_rest():
-        for load in loads[6:]:
-            load.wait()
-
     loads[0].wait()
     loads[1].wait()
+    for comp in range(3):
+        left, right = states([vel[comp, row] for row in range(ROWS)])
+        for piece in range(GROUP):
+            x1_send[0, piece, comp] = pack(left, right, piece)
     build_columns()
-    smooth(vel, 0, pass_tokens, load_rest, wait_tokens, nothing, nothing, keep_smoothed)
-
-    line_send(lambda comp, row: smoothed[comp, row], 0)
+    pass_tokens()
+    pieces_send(x1_send, x1_recv, x1_ss, x1_rs, 0)
+    line_send(lambda comp, row: vel[comp, row], 0)
+    x1_recv[0, member] = x1_send[0, member]
+    build_weights()
+    for load in loads[6:]:
+        load.wait()
+
+    def keep_along(comp, row, value):
+        along_y[comp, row] = value
+
+    line_local(lambda comp, row: vel[comp, row], 0, keep_along)
+    pieces_wait(x1_send, x1_recv, x1_ss, x1_rs, 0)
+    wait_tokens()
+
+    def first_piece(source, comp):
+        return x1_recv[0, source, comp]
+
+    ring_send(0, first_piece)
+    line_receive(0, lambda comp, row: along_y[comp, row], keep_along)
+    for comp in range(3):
+        for row, value in enumerate(local_rows([vel[comp, row] for row in range(ROWS)])):
+            smoothed[comp, row] = value
+        for row, value in enumerate(local_rows([along_y[comp, row] for row in range(ROWS)])):
+            feats[row, 8 * comp:8 * comp + 8, :] = value
+    ring_state = ring_receive(0, nothing)
+    for step in (2, 1, 3, 0):
+        other = in_group(step)
+        for comp in range(3):
+            tile = back_piece(ring_state, first_piece, other, comp)
+            x3_send[0, other, comp] = tile
+            project(0, other, comp, tile)
+    pieces_send(x3_send, x3_recv, x3_ss, x3_rs, 0)
+    plane_rows_send(0)
+    x3_recv[0, member] = x3_send[0, member]
+    pieces_wait(x3_send, x3_recv, x3_ss, x3_rs, 0)
+    for comp in range(3):
+        left, right = unpack([x3_recv[0, piece, comp] for piece in range(GROUP)])
+        for row in range(ROWS):
+            smoothed[comp, row] += scalar(LEFT + row) * left + scalar(RIGHT + row) * right
     along_z = depth_apply(smoothed[...].reshape(96, 256), 0)
     for comp in range(3):
         for row in range(ROWS):
             start = (comp * ROWS + row) * 8
             feats[row, 24 + 8 * comp:32 + 8 * comp, :] = along_z[start:start + 8]
-
-    def store_feature(comp, row, value):
-        feats[row, 8 * comp:8 * comp + 8, :] = value
-
-    line_local(lambda comp, row: smoothed[comp, row], 0, store_feature)
-    line_receive(0, lambda comp, row: feats[row, 8 * comp:8 * comp + 8, :], store_feature)
+    plane_rows_wait(0)
+    for comp in range(3):
+        left, right = unpack([
+            own_block(0, x3_recv[0, piece, comp]) + from_plane(0, piece, comp) for piece in range(GROUP)
+        ])
+        for row in range(ROWS):
+            feats[row, 8 * comp:8 * comp + 8, :] += scalar(LEFT + row) * left + scalar(RIGHT + row) * right
 
     def outward(row):
         parts = [STEP_SIZE * cot[comp, row] for comp in range(3)]
@@ -490,17 +593,32 @@
 
     lax.fori_loop(0, ROWS, closure, 0)
 
-    line_send(lambda comp, row: gfeats[row, 8 * comp:8 * comp + 8, :], 1)
+    def grad_along_y(comp, row):
+        return gfeats[row, 8 * comp:8 * comp + 8, :]
+
     back_in = jnp.concatenate(
         [gfeats[row, 24 + 8 * comp:32 + 8 * comp, :] for comp in range(3) for row in range(ROWS)], axis=0
     )
     along_z = depth_apply(back_in, 1)
-
-    def add_depth(comp, row, value):
-        start = (comp * ROWS + row) * 8
-        pulled[comp, row] = value + along_z[start:start + 8]
-
-    line_local(lambda comp, row: gfeats[row, 8 * comp:8 * comp + 8, :], 1, add_depth)
+    for comp in range(3):
+        left_y, right_y = states([grad_along_y(comp, row) for row in range(ROWS)])
+        starts = [(comp * ROWS + row) * 8 for row in range(ROWS)]
+        left_z, right_z = states([along_z[start:start + 8] for start in starts])
+        for piece in range(GROUP):
+            tile = pack(left_y, right_y, piece)
+            x1_send[1, piece, comp] = own_block(1, tile) + pack(left_z, right_z, piece)
+            project(1, piece, comp, tile)
+        for row in range(ROWS):
+            pulled[comp, row] = along_z[starts[row]:starts[row] + 8]
+    pieces_send(x1_send, x1_recv, x1_ss, x1_rs, 1)
+    plane_rows_send(1)
+    line_send(grad_along_y, 1)
+    x1_recv[1, member] = x1_send[1, member]
+
+    def keep_pulled(comp, row, value):
+        pulled[comp, row] = value
+
+    line_local(grad_along_y, 1, lambda comp, row, value: keep_pulled(comp, row, pulled[comp, row] + value))
 
     def forces_and_sums(row, carry):
         hidden_high, hidden_low = split(hidden_buf[row])
@@ -520,12 +638,9 @@
         sums[56:88, :] += both[0:32] + both[32:64] + rest
         return carry
 
-    def first_sums():
+    def partial_sums():
         sums[...] = jnp.zeros((88, 512), F32)
-        lax.fori_loop(0, ROWS // 2, forces_and_sums, 0)
-
-    def last_sums():
-        lax.fori_loop(ROWS // 2, ROWS, forces_and_sums, 0)
+        lax.fori_loop(0, ROWS, forces_and_sums, 0)
         same = lax.bitwise_and(iota((88, 512), 0), 7) == lax.bitwise_and(iota((88, 512), 1), 7)
         gather = ones_where(lax.shift_right_logical(iota((512, UNITS), 0), 3) == iota((512, UNITS), 1)).astype(BF16)
         high, low = split(jnp.where(same, sums[...], 0.0))
@@ -571,30 +686,45 @@
             total = total + p3[other]
         totals[...] = total * (1.0 / float(256 * 64 * 256))
 
-    first_sums()
-
-    def keep_pulled(comp, row, value):
-        pulled[comp, row] = value
-
-    line_receive(1, lambda comp, row: pulled[comp, row], keep_pulled)
-
-    def keep_gradient(comp, row, value):
-        gvel[comp, row] = cot[comp, row] + value
-
     stores = [
         pltpu.make_async_copy(nvel, new_velocity, local_sem.at[0]),
         pltpu.make_async_copy(gvel, grad_velocity, local_sem.at[1]),
         pltpu.make_async_copy(totals, grad_weights, local_sem.at[2]),
     ]
-
-    def store_velocity():
-        stores[0].start()
-        sum_line()
-
-    smooth(pulled, 1, nothing, last_sums, nothing, store_velocity, sum_group, keep_gradient)
+    partial_sums()
+    stores[0].start()
+    pieces_wait(x1_send, x1_recv, x1_ss, x1_rs, 1)
+    plane_rows_wait(1)
+    for source in range(GROUP):
+        for comp in range(3):
+            state[source, comp] = x1_recv[1, source, comp] + from_plane(1, source, comp)
+
+    def second_piece(source, comp):
+        return state[source, comp]
+
+    ring_send(1, second_piece)
+    line_receive(1, lambda comp, row: pulled[comp, row], keep_pulled)
+    for comp in range(3):
+        for row, value in enumerate(local_rows([pulled[comp, row] for row in range(ROWS)])):
+            gvel[comp, row] = cot[comp, row] + value
+    sum_line()
+    ring_state = ring_receive(1, sum_group)
+    for step in (2, 1, 3, 0):
+        other = in_group(step)
+        for comp in range(3):
+            x3_send[1, other, comp] = back_piece(ring_state, second_piece, other, comp)
+    pieces_send(x3_send, x3_recv, x3_ss, x3_rs, 1)
+    x3_recv[1, member] = x3_send[1, member]
+    pieces_wait(x3_send, x3_recv, x3_ss, x3_rs, 1)
+    for comp in range(3):
+        left, right = unpack([x3_recv[1, piece, comp] for piece in range(GROUP)])
+        for row in range(ROWS):
+            gvel[comp, row] += scalar(LEFT + row) * left + scalar(RIGHT + row) * right
     stores[1].start()
     sum_ring()
     stores[2].start()
+    plane_rows_drain(0)
+    plane_rows_drain(1)
     for copy in sent:
         copy.wait_send()
     for store in stores:
@@ -632,6 +762,7 @@
             pltpu.VMEM(field, F32),
             pltpu.VMEM(field, F32),
             pltpu.VMEM(field, F32),
+            pltpu.VMEM(field, F32),
             pltpu.VMEM((ROWS, 48, 256), F32),
             pltpu.VMEM((ROWS, 48, 256), F32),
             pltpu.VMEM(field, F32),
@@ -649,14 +780,18 @@
             pltpu.VMEM((ROWS, 2, 512, 256), BF16),
             pltpu.VMEM((88, 512), F32),
             pltpu.VMEM((8, 128), F32),
-            pltpu.VMEM((2, GROUP, 2, 3, 2, 256), F32),
-            pltpu.VMEM((2, GROUP, 2, 3, 2, 256), F32),
-            pltpu.VMEM((2, 2, 3, 2, 256), F32),
-            pltpu.VMEM((2, RING, 3, 2, 256), F32),
-            pltpu.VMEM((2, GROUP, 2, 3, 2, 256), F32),
-            pltpu.VMEM((2, GROUP, 2, 3, 2, 256), F32),
+            pltpu.VMEM((2, GROUP, 3, 8, 128), F32),
+            pltpu.VMEM((2, GROUP, 3, 8, 128), F32),
+            pltpu.VMEM((GROUP, 3, 8, 128), F32),
+            pltpu.VMEM((2, 2, 3, 4, 128), F32),
+            pltpu.VMEM((2, RING, 3, 4, 128), F32),
+            pltpu.VMEM((2, GROUP, 3, 8, 128), F32),
+            pltpu.VMEM((2, GROUP, 3, 8, 128), F32),
+            pltpu.VMEM((2, GROUP, 4, 3, 128), F32),
+            pltpu.VMEM((2, GROUP, LINE - 1, 3, 128), F32),
+            pltpu.VMEM((2, GROUP, 2, 3, 128), F32),
             pltpu.VMEM((2, 4, 3, ROWS, 256), F32),
-            pltpu.VMEM((2, LINE, 3, ROWS, 256), F32),
+            pltpu.VMEM((2, LINE - 1, 3, ROWS, 256), F32),
             pltpu.VMEM((2, 2, 3, ROWS, 256), F32),
             pltpu.VMEM((LINE, 8, 128), F32),
             pltpu.VMEM((GROUP, 8, 128), F32),
@@ -666,7 +801,8 @@
             dma((2, GROUP)), dma((2, GROUP)),
             dma((2, RING)), dma((2, RING)),
             dma((2, GROUP)), dma((2, GROUP)),
-            dma((2, LINE)), dma((2, LINE)),
+            dma((2,)), dma((2,)), dma((2,)), dma((2,)),
+            dma((2, LINE - 1)), dma((2, LINE - 1)),
             dma((2, 2)), dma((2, 2)),
             dma((LINE,)), dma((LINE,)),
             dma((GROUP,)), dma((GROUP,)),

time: 59.1 us -> 57.4 us (0.971)
  Pallas kernels: 58.3 us -> 56.5 us
    pallas_call x1, Pallas kernels: 56.6 us -> 54.8 us  [local(): pl.pallas_call(kernel, out_shape=(jax.ShapeDtypeStruct(field, F32), jax.S...]
where the time goes in v3:
time: 57.4 us; the launch traced here: 57.1 us
  Pallas kernels  56.5 us (98%)
  between operations  0.64 us (1%)
    pallas_call x1, Pallas kernels, local(): pl.pallas_call(kernel, out_shape=(jax.ShapeDtypeStruct(field, F32), jax.S...  54.8 us
    pallas_call x1, Pallas kernels, local(): pl.pallas_call(finish, out_shape=(jax.ShapeDtypeStruct(field, F32), jax.S...  1.64 us

profile of v3, /device:TPU:2, one launch (start us, length us, event | category | flops | bytes accessed | tf_op | source)
XLA Modules:
  0.0 57.1 jit_solution(1051302796126046910)
XLA Ops:
  0.6 54.8 %closure_step.1 = (f32[3,4,8,256]{3,2,1,0:T(8,128)}, f32[3,4,8,256]{3,2,1,0:T(8,128)}, f32[8,128]{1,0:T(8,128)}) custom-call(f32[3,4,8,256]{3,2,1,0:T(8,128)} %velocity.1, f32[3,4,8,256]{3,2,1,0:T(8,128)} %cotangent.1, f32[6,64]{1,0:T(8,128)} %weight_in.1, f32[1,64]{1,0:T(1,128)} %bitcast.5, f32[3,64]{1,0:T(4,128)} %bitcast.4, ...), custom_call_target="tpu_custom_call" | custom-call | tf_op jit(solution)/shard_map/closure_step/pallas_call | solution.py:749
  55.5 1.6 %finish.1 = (f32[3,4,8,256]{3,2,1,0:T(8,128)}, f32[3,4,8,256]{3,2,1,0:T(8,128)}, f32[6,64]{1,0:T(8,128)}, f32[1,64]{1,0:T(1,128)}, f32[3,64]{1,0:T(4,128)}) custom-call(f32[3,4,8,256]{3,2,1,0:T(8,128)} %get-tuple-element.13.new_velocity_in, f32[3,4,8,256]{3,2,1,0:T(8,128)} %get-tuple-element.14.grad_velocity_in, f32[8,128]{1,0:T(8,128)} %get-tuple-element.15.grads), custom_call_target="tpu_custom_call" | custom-call | tf_op jit(solution)/shard_map/finish/pallas_call | solution.py:818

commit v4 on v3

--- a/solution.py
+++ b/solution.py
@@ -22,6 +22,7 @@
 LINE = 8
 ROWS = 4
 UNITS = 64
+RESERVED = 66300000
 
 UP_W, DOWN_W, UP_C, DOWN_C, RING_L, RING_R, BACK_L, BACK_R, LOCAL, LEFT, RIGHT = (
     0, 4, 8, 12, 16, 32, 48, 68, 88, 104, 108
@@ -158,9 +159,9 @@
 def kernel(
     velocity, cotangent, weight_in, bias_in, weight_out, x_table, y_table, z_table,
     new_velocity, grad_velocity, grad_weights,
-    w_in, w_bias, w_out, vel, cot, along_y, smoothed, feats, gfeats, pulled, nvel, gvel,
+    w_in, w_bias, w_out, vel, cot, along_y, smoothed, feats, gfeats, pulled,
     scalars, columns, tall, ztab,
-    left_lhs, back_lhs, force_lhs, rhs, hidden_buf, pre_buf, sums, totals,
+    left_lhs, back_lhs, force_lhs, rhs, hidden_buf, pre_buf, sums,
     x1_send, x1_recv, state, x2_send, x2_recv, x3_send, x3_recv, plane_send, plane_recv, plane_edge,
     y_send, y_recv, y_edge,
     p1, p2, p3,
@@ -356,12 +357,10 @@
                 x2_ss.at[order, other], x2_rs.at[order, ring], ring_device(other),
             )
 
-    def ring_receive(order, midway):
+    def ring_receive(order):
         left = jnp.zeros((3, 4, 128), F32)
         right = jnp.zeros((3, 4, 128), F32)
         for step in (1, 15, 2, 14, 3, 13, 4, 12, 5, 11, 6, 10, 7, 9, 8):
-            if step == 5:
-                midway()
             other = in_ring(step)
             remote(
                 x2_send.at[order, 0], x2_recv.at[order, other],
@@ -504,9 +503,6 @@
         for kind in range(2):
             pl.semaphore_wait(token.at[kind], 1)
 
-    def nothing():
-        pass
-
     loads[0].wait()
     loads[1].wait()
     for comp in range(3):
@@ -539,7 +535,7 @@
             smoothed[comp, row] = value
         for row, value in enumerate(local_rows([along_y[comp, row] for row in range(ROWS)])):
             feats[row, 8 * comp:8 * comp + 8, :] = value
-    ring_state = ring_receive(0, nothing)
+    ring_state = ring_receive(0)
     for step in (2, 1, 3, 0):
         other = in_group(step)
         for comp in range(3):
@@ -612,20 +608,25 @@
             pulled[comp, row] = along_z[starts[row]:starts[row] + 8]
     pieces_send(x1_send, x1_recv, x1_ss, x1_rs, 1)
     plane_rows_send(1)
-    line_send(grad_along_y, 1)
     x1_recv[1, member] = x1_send[1, member]
 
     def keep_pulled(comp, row, value):
         pulled[comp, row] = value
 
-    line_local(grad_along_y, 1, lambda comp, row, value: keep_pulled(comp, row, pulled[comp, row] + value))
-
-    def forces_and_sums(row, carry):
+    def line_part():
+        line_send(grad_along_y, 1)
+        line_local(grad_along_y, 1, lambda comp, row, value: keep_pulled(comp, row, pulled[comp, row] + value))
+
+    def forces(row, carry):
         hidden_high, hidden_low = split(hidden_buf[row])
         both = matmul(force_lhs[...], hidden_high)
         forcing = both[0:32] + both[32:64] + matmul(force_lhs[0:32, :], hidden_low)
         for comp in range(3):
-            nvel[comp, row] = vel[comp, row] + STEP_SIZE * forcing[8 * comp:8 * comp + 8]
+            new_velocity[comp, row] = vel[comp, row] + STEP_SIZE * forcing[8 * comp:8 * comp + 8]
+        return carry
+
+    def row_sums(row, carry):
+        hidden_high, hidden_low = split(hidden_buf[row])
         feature_high, feature_low = split(feats[row])
         ones = jnp.ones((16, 256), BF16)
         both = matmul_nt(jnp.concatenate([feature_high, ones, feature_low], axis=0), pre_buf[row, 0])
@@ -640,7 +641,7 @@
 
     def partial_sums():
         sums[...] = jnp.zeros((88, 512), F32)
-        lax.fori_loop(0, ROWS, forces_and_sums, 0)
+        lax.fori_loop(0, ROWS, row_sums, 0)
         same = lax.bitwise_and(iota((88, 512), 0), 7) == lax.bitwise_and(iota((88, 512), 1), 7)
         gather = ones_where(lax.shift_right_logical(iota((512, UNITS), 0), 3) == iota((512, UNITS), 1)).astype(BF16)
         high, low = split(jnp.where(same, sums[...], 0.0))
@@ -684,15 +685,10 @@
         total = p3[0]
         for other in range(1, RING):
             total = total + p3[other]
-        totals[...] = total * (1.0 / float(256 * 64 * 256))
-
-    stores = [
-        pltpu.make_async_copy(nvel, new_velocity, local_sem.at[0]),
-        pltpu.make_async_copy(gvel, grad_velocity, local_sem.at[1]),
-        pltpu.make_async_copy(totals, grad_weights, local_sem.at[2]),
-    ]
+        grad_weights[...] = total * (1.0 / float(256 * 64 * 256))
+
     partial_sums()
-    stores[0].start()
+    line_part()
     pieces_wait(x1_send, x1_recv, x1_ss, x1_rs, 1)
     plane_rows_wait(1)
     for source in range(GROUP):
@@ -703,12 +699,14 @@
         return state[source, comp]
 
     ring_send(1, second_piece)
+    sum_line()
+    lax.fori_loop(0, ROWS, forces, 0)
     line_receive(1, lambda comp, row: pulled[comp, row], keep_pulled)
     for comp in range(3):
         for row, value in enumerate(local_rows([pulled[comp, row] for row in range(ROWS)])):
-            gvel[comp, row] = cot[comp, row] + value
-    sum_line()
-    ring_state = ring_receive(1, sum_group)
+            grad_velocity[comp, row] = cot[comp, row] + value
+    sum_group()
+    ring_state = ring_receive(1)
     for step in (2, 1, 3, 0):
         other = in_group(step)
         for comp in range(3):
@@ -719,26 +717,28 @@
     for comp in range(3):
         left, right = unpack([x3_recv[1, piece, comp] for piece in range(GROUP)])
         for row in range(ROWS):
-            gvel[comp, row] += scalar(LEFT + row) * left + scalar(RIGHT + row) * right
-    stores[1].start()
+            grad_velocity[comp, row] += scalar(LEFT + row) * left + scalar(RIGHT + row) * right
     sum_ring()
-    stores[2].start()
     plane_rows_drain(0)
     plane_rows_drain(1)
     for copy in sent:
         copy.wait_send()
-    for store in stores:
-        store.wait()
-
-
-def finish(new_velocity_in, grad_velocity_in, grads, new_velocity, grad_velocity, grad_in, grad_bias, grad_out_t):
-    new_velocity[...] = new_velocity_in[...]
-    grad_velocity[...] = grad_velocity_in[...]
+
+
+def finish(new_velocity_in, grad_velocity_in, grads, new_velocity, grad_velocity, grad_in, grad_bias, grad_out_t, sems):
+    copies = [
+        pltpu.make_async_copy(new_velocity_in, new_velocity, sems.at[0]),
+        pltpu.make_async_copy(grad_velocity_in, grad_velocity, sems.at[1]),
+    ]
+    for copy in copies:
+        copy.start()
     front = grads[:, 0:UNITS]
     grad_in[...] = front[0:6]
     grad_bias[...] = front[6:7]
     grad_out_t[0:1] = front[7:8]
     grad_out_t[1:3] = grads[0:2, UNITS:2 * UNITS]
+    for copy in copies:
+        copy.wait()
 
 
 def local(velocity, cotangent, weight_in, bias_in, weight_out):
@@ -749,12 +749,12 @@
     mid = pl.pallas_call(
         kernel,
         out_shape=(
-            jax.ShapeDtypeStruct(field, F32),
-            jax.ShapeDtypeStruct(field, F32),
-            jax.ShapeDtypeStruct((8, 128), F32),
+            pltpu.VMEM(field, F32),
+            pltpu.VMEM(field, F32),
+            pltpu.VMEM((8, 128), F32),
         ),
         in_specs=[anywhere] * 8,
-        out_specs=(anywhere, anywhere, anywhere),
+        out_specs=(whole, whole, whole),
         scratch_shapes=[
             pltpu.VMEM((6, UNITS), F32),
             pltpu.VMEM((1, UNITS), F32),
@@ -765,8 +765,6 @@
             pltpu.VMEM(field, F32),
             pltpu.VMEM((ROWS, 48, 256), F32),
             pltpu.VMEM((ROWS, 48, 256), F32),
-            pltpu.VMEM(field, F32),
-            pltpu.VMEM(field, F32),
             pltpu.VMEM(field, F32),
             pltpu.SMEM((1, 128), F32),
             pltpu.VMEM((8, 128), F32),
@@ -779,7 +777,6 @@
             pltpu.VMEM((ROWS, 512, 256), F32),
             pltpu.VMEM((ROWS, 2, 512, 256), BF16),
             pltpu.VMEM((88, 512), F32),
-            pltpu.VMEM((8, 128), F32),
             pltpu.VMEM((2, GROUP, 3, 8, 128), F32),
             pltpu.VMEM((2, GROUP, 3, 8, 128), F32),
             pltpu.VMEM((GROUP, 3, 8, 128), F32),
@@ -808,7 +805,7 @@
             dma((GROUP,)), dma((GROUP,)),
             dma((RING,)), dma((RING,)),
         ],
-        compiler_params=pltpu.CompilerParams(collective_id=0, has_side_effects=True),
+        compiler_params=pltpu.CompilerParams(collective_id=0, has_side_effects=True, vmem_limit_bytes=RESERVED),
         name="closure_step",
     )(
         velocity, cotangent, weight_in, bias_in.reshape(1, UNITS), weight_out.T,
@@ -825,7 +822,9 @@
             jax.ShapeDtypeStruct((3, UNITS), F32),
         ),
         in_specs=[whole] * 3,
-        out_specs=(whole,) * 5,
+        out_specs=(anywhere, anywhere, whole, whole, whole),
+        scratch_shapes=[dma((2,))],
+        compiler_params=pltpu.CompilerParams(vmem_limit_bytes=1 << 20),
         name="finish",
     )(*mid)
     return outs[0], outs[1], outs[2], outs[3].reshape(UNITS), outs[4].T

time: 57.4 us -> 52.7 us (0.918)
  the two profiles are of different devices: /device:TPU:2 before, /device:TPU:1 now
where the time goes in v4:
time: 52.7 us; the launch traced here: 52.6 us
  Pallas kernels  51.9 us (98%)
  between operations  0.64 us (1%)
    pallas_call x1, Pallas kernels, local(): pl.pallas_call(kernel, out_shape=(pltpu.VMEM(field, F32), pltpu.VMEM(fiel...  50.7 us
    pallas_call x1, Pallas kernels, local(): pl.pallas_call(finish, out_shape=(jax.ShapeDtypeStruct(field, F32), jax.S...  1.29 us

profile of v4, /device:TPU:1, one launch (start us, length us, event | category | flops | bytes accessed | tf_op | source)
XLA Modules:
  0.0 52.6 jit_solution(6130569432215307255)
XLA Ops:
  0.6 50.7 %closure_step.1 = (f32[3,4,8,256]{3,2,1,0:T(8,128)S(1)}, f32[3,4,8,256]{3,2,1,0:T(8,128)S(1)}, f32[8,128]{1,0:T(8,128)S(1)}) custom-call(f32[3,4,8,256]{3,2,1,0:T(8,128)} %velocity.1, f32[3,4,8,256]{3,2,1,0:T(8,128)} %cotangent.1, f32[6,64]{1,0:T(8,128)} %weight_in.1, f32[1,64]{1,0:T(1,128)} %bitcast.5, f32[3,64]{1,0:T(4,128)} %bitcast.4, ...), custom_call_target="tpu_custom_call" | custom-call | tf_op jit(solution)/shard_map/closure_step/pallas_call | solution.py:749
  51.3 1.3 %finish.1 = (f32[3,4,8,256]{3,2,1,0:T(8,128)}, f32[3,4,8,256]{3,2,1,0:T(8,128)}, f32[6,64]{1,0:T(8,128)}, f32[1,64]{1,0:T(1,128)}, f32[3,64]{1,0:T(4,128)}) custom-call(f32[3,4,8,256]{3,2,1,0:T(8,128)S(1)} %get-tuple-element.13.new_velocity_in, f32[3,4,8,256]{3,2,1,0:T(8,128)S(1)} %get-tuple-element.14.grad_velocity_in, f32[8,128]{1,0:T(8,128)S(1)} %get-tuple-element.15.grads), custom_call_target="tpu_custom_call" | custom-call | tf_op jit(solution)/shard_map/finish/pallas_call | solution.py:815

commit v5 on v4

--- a/solution.py
+++ b/solution.py
@@ -161,7 +161,7 @@
     new_velocity, grad_velocity, grad_weights,
     w_in, w_bias, w_out, vel, cot, along_y, smoothed, feats, gfeats, pulled,
     scalars, columns, tall, ztab,
-    left_lhs, back_lhs, force_lhs, rhs, hidden_buf, pre_buf, sums,
+    left_lhs, out_lhs, back_lhs, force_lhs, rhs, pulled_out, hidden_buf, pre_buf, sums,
     x1_send, x1_recv, state, x2_send, x2_recv, x3_send, x3_recv, plane_send, plane_recv, plane_edge,
     y_send, y_recv, y_edge,
     p1, p2, p3,
@@ -197,13 +197,10 @@
 
     barrier = pltpu.get_barrier_semaphore()
     half = RING // 4
-    near = list(range(1, half + 1)) + list(range(RING - half, RING))
     partners = (
-        [ring_device(in_ring(step)) for step in near]
-        + [
-            plane_device(in_group(step), in_line(along))
-            for step in range(GROUP) for along in range(LINE) if step or along
-        ]
+        [ring_device(in_ring(step)) for step in (4, 12, 3, 13, 2, 14, 1, 15)]
+        + [line_device(in_line(step)) for step in range(1, LINE)]
+        + [group_device(in_group(step)) for step in range(1, GROUP)]
     )
     for partner in partners:
         pl.semaphore_signal(barrier, inc=1, device_id=partner, device_id_type=MESH)
@@ -234,6 +231,11 @@
         if drain:
             sent.append(copy)
 
+    def drain(count):
+        for copy in sent[:count]:
+            copy.wait_send()
+        del sent[:count]
+
     def scalar(index):
         return scalars[0, index]
 
@@ -246,27 +248,28 @@
         bias = w_bias[...]
         b_high, b_low = split(bias)
         b_rest = bias - b_high.astype(F32) - b_low.astype(F32)
-        row = iota((8, 256), 0)
-        col = iota((8, 256), 1)
+        row = iota((8, 160), 0)
+        col = iota((8, 160), 1)
         field = lax.shift_right_logical(col, 3)
         pick_high = ones_where(((field == row) | (field == row + 6)) & (row < 6)).astype(BF16)
         pick_low = ones_where((field == row + 12) & (row < 6)).astype(BF16)
         spread_high = matmul_nt(spread, w_high).astype(BF16)
         spread_low = matmul_nt(spread, w_low).astype(BF16)
         top = matmul(spread_high, pick_high[0:6]) + matmul(spread_low, pick_low[0:6])
-        same = lax.bitwise_and(iota((512, 256), 0), 7) == lax.bitwise_and(iota((512, 256), 1), 7)
+        same = lax.bitwise_and(iota((512, 160), 0), 7) == lax.bitwise_and(iota((512, 160), 1), 7)
         top = jnp.where(same, top, 0.0)
         biases = jnp.concatenate([b_high.astype(F32), b_low.astype(F32), b_rest, jnp.zeros((5, UNITS), F32)], axis=0)
         spread_bias = matmul_nt(spread, biases.astype(BF16)).astype(BF16)
-        top = top + matmul(spread_bias, ones_where(col == row + 240).astype(BF16))
-        left_lhs[0:512, :] = top.astype(BF16)
+        top = top + matmul(spread_bias, ones_where(col == row + 144).astype(BF16))
+        left_lhs[...] = top.astype(BF16)
         o_high, o_low = split(w_out[...])
-        pick_high = ones_where(((field == row + 18) | (field == row + 22)) & (row < 3)).astype(BF16)
-        pick_low = ones_where((field == row + 26) & (row < 3)).astype(BF16)
+        row, field, same = row[:, 0:96], field[:, 0:96], same[:, 0:96]
+        pick_high = ones_where(((field == row) | (field == row + 4)) & (row < 3)).astype(BF16)
+        pick_low = ones_where((field == row + 8) & (row < 3)).astype(BF16)
         spread_oh = matmul_nt(spread, o_high).astype(BF16)
         spread_ol = matmul_nt(spread, o_low).astype(BF16)
         bottom = matmul(spread_oh, pick_high[0:3]) + matmul(spread_ol, pick_low[0:3])
-        left_lhs[512:1024, :] = jnp.where(same, bottom, 0.0).astype(BF16)
+        out_lhs[...] = jnp.where(same, bottom, 0.0).astype(BF16)
 
         same_t = lax.bitwise_and(iota((96, 512), 0), 7) == lax.bitwise_and(iota((96, 512), 1), 7)
         row = lax.shift_right_logical(iota((96, 8), 0), 3)
@@ -389,23 +392,24 @@
     def project(order, other, comp, tile):
         out = sum(tall[24 * order + 8 + col] * tile[col:col + 1] for col in range(8))
         for kind in range(4):
-            plane_send[order, other, kind, comp:comp + 1, :] = out[kind:kind + 1]
+            plane_send[order, other, kind // 2, kind % 2, comp:comp + 1, :] = out[kind:kind + 1]
 
     def plane_rows_send(order):
         for step in (2, 1, 3, 0):
             other = in_group(step)
             for along in (4, 5, 3, 6, 2, 7, 1):
                 place = in_line(along)
-                kind = jnp.where(place > gy, 1, 3)
-                send(
-                    plane_send.at[order, other, kind], plane_recv.at[order, member, along - 1],
-                    plane_ss.at[order], plane_rs.at[order], plane_device(other, place), drain=False,
-                )
-            for kind, along in ((0, 1), (1, LINE - 1)):
-                send(
-                    plane_send.at[order, other, 2 * kind], plane_edge.at[order, member, kind],
-                    edge_ss.at[order], edge_rs.at[order], plane_device(other, in_line(along)), drain=False,
-                )
+                side = jnp.where(place > gy, 0, 1)
+                if along in (1, LINE - 1):
+                    send(
+                        plane_send.at[order, other, side], plane_edge.at[order, member, 0 if along == 1 else 1],
+                        edge_ss.at[order], edge_rs.at[order], plane_device(other, place), drain=False,
+                    )
+                else:
+                    send(
+                        plane_send.at[order, other, side, 1], plane_recv.at[order, member, along - 2],
+                        plane_ss.at[order], plane_rs.at[order], plane_device(other, place), drain=False,
+                    )
 
     def plane_rows_all(order):
         device = plane_device(in_group(1), in_line(1))
@@ -423,10 +427,14 @@
             copy.wait_send()
 
     def from_plane(order, source, comp):
-        total = tall[48] * plane_edge[order, source, 0, comp:comp + 1, :]
-        total = total + tall[49] * plane_edge[order, source, 1, comp:comp + 1, :]
-        for along in range(1, LINE):
-            total = total + tall[24 * order + 16 + along] * plane_recv[order, source, along - 1, comp:comp + 1, :]
+        def row(ref, *index):
+            return ref[(order, source) + index + (slice(comp, comp + 1),)]
+
+        factor = 24 * order + 16
+        total = tall[48] * row(plane_edge, 0, 0) + tall[factor + 1] * row(plane_edge, 0, 1)
+        total = total + tall[49] * row(plane_edge, 1, 0) + tall[factor + LINE - 1] * row(plane_edge, 1, 1)
+        for along in range(2, LINE - 1):
+            total = total + tall[factor + along] * row(plane_recv, along - 2)
         return total
 
     def own_block(order, tile):
@@ -499,8 +507,13 @@
                 token.at[kind], inc=1, device_id=ring_device(in_ring(step)), device_id_type=MESH
             )
 
-    def wait_tokens():
-        for kind in range(2):
+        for step in range(1, GROUP):
+            pl.semaphore_signal(
+                token.at[1 + step], inc=1, device_id=group_device(in_group(step)), device_id_type=MESH
+            )
+
+    def wait_tokens(first, last):
+        for kind in range(first, last):
             pl.semaphore_wait(token.at[kind], 1)
 
     loads[0].wait()
@@ -523,7 +536,7 @@
 
     line_local(lambda comp, row: vel[comp, row], 0, keep_along)
     pieces_wait(x1_send, x1_recv, x1_ss, x1_rs, 0)
-    wait_tokens()
+    wait_tokens(0, 2)
 
     def first_piece(source, comp):
         return x1_recv[0, source, comp]
@@ -535,6 +548,18 @@
             smoothed[comp, row] = value
         for row, value in enumerate(local_rows([along_y[comp, row] for row in range(ROWS)])):
             feats[row, 8 * comp:8 * comp + 8, :] = value
+    def outward(row):
+        parts = [STEP_SIZE * cot[comp, row] for comp in range(3)]
+        return jnp.concatenate(parts + [jnp.zeros((8, 256), F32)], axis=0)
+
+    def grad_of_hidden(row, carry):
+        out_high, out_low = split(outward(row))
+        pulled_out[row] = matmul(out_lhs[...], jnp.concatenate([out_high, out_low, out_high], axis=0))
+        rhs[row, 144:160, :] = jnp.ones((16, 256), BF16)
+        return carry
+
+    lax.fori_loop(0, ROWS, grad_of_hidden, 0)
+    wait_tokens(2, 1 + GROUP)
     ring_state = ring_receive(0)
     for step in (2, 1, 3, 0):
         other = in_group(step)
@@ -542,8 +567,8 @@
             tile = back_piece(ring_state, first_piece, other, comp)
             x3_send[0, other, comp] = tile
             project(0, other, comp, tile)
+    plane_rows_send(0)
     pieces_send(x3_send, x3_recv, x3_ss, x3_rs, 0)
-    plane_rows_send(0)
     x3_recv[0, member] = x3_send[0, member]
     pieces_wait(x3_send, x3_recv, x3_ss, x3_rs, 0)
     for comp in range(3):
@@ -563,51 +588,45 @@
         for row in range(ROWS):
             feats[row, 8 * comp:8 * comp + 8, :] += scalar(LEFT + row) * left + scalar(RIGHT + row) * right
 
-    def outward(row):
-        parts = [STEP_SIZE * cot[comp, row] for comp in range(3)]
-        return jnp.concatenate(parts + [jnp.zeros((8, 256), F32)], axis=0)
-
-    def closure(row, carry):
+    def closure(row):
         feature_high, feature_low = split(feats[row])
-        rhs[0:48, :] = feature_high
-        rhs[48:96, :] = feature_low
-        rhs[96:144, :] = feature_high
-        out_high, out_low = split(outward(row))
-        rhs[144:176, :] = out_high
-        rhs[176:208, :] = out_low
-        rhs[208:240, :] = out_high
-        rhs[240:256, :] = jnp.ones((16, 256), BF16)
-        hidden = jnp.tanh(matmul(left_lhs[0:512, :], rhs[...]))
-        grad_pre = matmul(left_lhs[512:1024, :], rhs[...]) * (1.0 - hidden * hidden)
+        rhs[row, 0:48, :] = feature_high
+        rhs[row, 48:96, :] = feature_low
+        rhs[row, 96:144, :] = feature_high
+        hidden = jnp.tanh(matmul(left_lhs[...], rhs[row]))
+        grad_pre = pulled_out[row] * (1.0 - hidden * hidden)
         pre_high, pre_low = split(grad_pre)
         hidden_buf[row] = hidden
         pre_buf[row, 0] = pre_high
         pre_buf[row, 1] = pre_low
         both = matmul(back_lhs[...], pre_high)
         gfeats[row] = both[0:48] + both[48:96] + matmul(back_lhs[0:48, :], pre_low)
-        return carry
-
-    lax.fori_loop(0, ROWS, closure, 0)
+
+    for row in range(ROWS):
+        closure(row)
 
     def grad_along_y(comp, row):
         return gfeats[row, 8 * comp:8 * comp + 8, :]
 
+    packed = {}
+    for comp in range(3):
+        left, right = states([grad_along_y(comp, row) for row in range(ROWS)])
+        for piece in range(GROUP):
+            packed[piece, comp] = pack(left, right, piece)
+            project(1, piece, comp, packed[piece, comp])
+    plane_rows_send(1)
     back_in = jnp.concatenate(
         [gfeats[row, 24 + 8 * comp:32 + 8 * comp, :] for comp in range(3) for row in range(ROWS)], axis=0
     )
     along_z = depth_apply(back_in, 1)
     for comp in range(3):
-        left_y, right_y = states([grad_along_y(comp, row) for row in range(ROWS)])
         starts = [(comp * ROWS + row) * 8 for row in range(ROWS)]
-        left_z, right_z = states([along_z[start:start + 8] for start in starts])
+        left, right = states([along_z[start:start + 8] for start in starts])
         for piece in range(GROUP):
-            tile = pack(left_y, right_y, piece)
-            x1_send[1, piece, comp] = own_block(1, tile) + pack(left_z, right_z, piece)
-            project(1, piece, comp, tile)
+            x1_send[1, piece, comp] = own_block(1, packed[piece, comp]) + pack(left, right, piece)
         for row in range(ROWS):
             pulled[comp, row] = along_z[starts[row]:starts[row] + 8]
     pieces_send(x1_send, x1_recv, x1_ss, x1_rs, 1)
-    plane_rows_send(1)
     x1_recv[1, member] = x1_send[1, member]
 
     def keep_pulled(comp, row, value):
@@ -698,6 +717,7 @@
     def second_piece(source, comp):
         return state[source, comp]
 
+    early = len(sent)
     ring_send(1, second_piece)
     sum_line()
     lax.fori_loop(0, ROWS, forces, 0)
@@ -706,6 +726,9 @@
         for row, value in enumerate(local_rows([pulled[comp, row] for row in range(ROWS)])):
             grad_velocity[comp, row] = cot[comp, row] + value
     sum_group()
+    drain(early)
+    plane_rows_drain(0)
+    plane_rows_drain(1)
     ring_state = ring_receive(1)
     for step in (2, 1, 3, 0):
         other = in_group(step)
@@ -719,10 +742,7 @@
         for row in range(ROWS):
             grad_velocity[comp, row] += scalar(LEFT + row) * left + scalar(RIGHT + row) * right
     sum_ring()
-    plane_rows_drain(0)
-    plane_rows_drain(1)
-    for copy in sent:
-        copy.wait_send()
+    drain(len(sent))
 
 
 def finish(new_velocity_in, grad_velocity_in, grads, new_velocity, grad_velocity, grad_in, grad_bias, grad_out_t, sems):
@@ -770,10 +790,12 @@
             pltpu.VMEM((8, 128), F32),
             pltpu.VMEM((50, 8, 128), F32),
             pltpu.VMEM((4, 256, 256), BF16),
-            pltpu.VMEM((1024, 256), BF16),
+            pltpu.VMEM((512, 160), BF16),
+            pltpu.VMEM((512, 96), BF16),
             pltpu.VMEM((96, 512), BF16),
             pltpu.VMEM((64, 512), BF16),
-            pltpu.VMEM((256, 256), BF16),
+            pltpu.VMEM((ROWS, 160, 256), BF16),
+            pltpu.VMEM((ROWS, 512, 256), F32),
             pltpu.VMEM((ROWS, 512, 256), F32),
             pltpu.VMEM((ROWS, 2, 512, 256), BF16),
             pltpu.VMEM((88, 512), F32),
@@ -784,16 +806,16 @@
             pltpu.VMEM((2, RING, 3, 4, 128), F32),
             pltpu.VMEM((2, GROUP, 3, 8, 128), F32),
             pltpu.VMEM((2, GROUP, 3, 8, 128), F32),
-            pltpu.VMEM((2, GROUP, 4, 3, 128), F32),
-            pltpu.VMEM((2, GROUP, LINE - 1, 3, 128), F32),
-            pltpu.VMEM((2, GROUP, 2, 3, 128), F32),
+            pltpu.VMEM((2, GROUP, 2, 2, 3, 128), F32),
+            pltpu.VMEM((2, GROUP, LINE - 3, 3, 128), F32),
+            pltpu.VMEM((2, GROUP, 2, 2, 3, 128), F32),
             pltpu.VMEM((2, 4, 3, ROWS, 256), F32),
             pltpu.VMEM((2, LINE - 1, 3, ROWS, 256), F32),
             pltpu.VMEM((2, 2, 3, ROWS, 256), F32),
             pltpu.VMEM((LINE, 8, 128), F32),
             pltpu.VMEM((GROUP, 8, 128), F32),
             pltpu.VMEM((RING, 8, 128), F32),
-            pltpu.SemaphoreType.REGULAR((2,)),
+            pltpu.SemaphoreType.REGULAR((1 + GROUP,)),
             dma((8,)),
             dma((2, GROUP)), dma((2, GROUP)),
             dma((2, RING)), dma((2, RING)),

time: 52.7 us -> 50.5 us (0.958)
  the two profiles are of different devices: /device:TPU:1 before, /device:TPU:2 now
where the time goes in v5:
time: 50.5 us; the launch traced here: 50.3 us
  Pallas kernels  49.7 us (98%)
  between operations  0.64 us (1%)
    pallas_call x1, Pallas kernels, local(): pl.pallas_call(kernel, out_shape=(pltpu.VMEM(field, F32), pltpu.VMEM(fiel...  48.4 us
    pallas_call x1, Pallas kernels, local(): pl.pallas_call(finish, out_shape=(jax.ShapeDtypeStruct(field, F32), jax.S...  1.29 us

profile of v5, /device:TPU:2, one launch (start us, length us, event | category | flops | bytes accessed | tf_op | source)
XLA Modules:
  0.0 50.3 jit_solution(7135199642331530420)
XLA Ops:
  0.6 48.4 %closure_step.1 = (f32[3,4,8,256]{3,2,1,0:T(8,128)S(1)}, f32[3,4,8,256]{3,2,1,0:T(8,128)S(1)}, f32[8,128]{1,0:T(8,128)S(1)}) custom-call(f32[3,4,8,256]{3,2,1,0:T(8,128)} %velocity.1, f32[3,4,8,256]{3,2,1,0:T(8,128)} %cotangent.1, f32[6,64]{1,0:T(8,128)} %weight_in.1, f32[1,64]{1,0:T(1,128)} %bitcast.5, f32[3,64]{1,0:T(4,128)} %bitcast.4, ...), custom_call_target="tpu_custom_call" | custom-call | tf_op jit(solution)/shard_map/closure_step/pallas_call | solution.py:769
  49.0 1.3 %finish.1 = (f32[3,4,8,256]{3,2,1,0:T(8,128)}, f32[3,4,8,256]{3,2,1,0:T(8,128)}, f32[6,64]{1,0:T(8,128)}, f32[1,64]{1,0:T(1,128)}, f32[3,64]{1,0:T(4,128)}) custom-call(f32[3,4,8,256]{3,2,1,0:T(8,128)S(1)} %get-tuple-element.13.new_velocity_in, f32[3,4,8,256]{3,2,1,0:T(8,128)S(1)} %get-tuple-element.14.grad_velocity_in, f32[8,128]{1,0:T(8,128)S(1)} %get-tuple-element.15.grads), custom_call_target="tpu_custom_call" | custom-call | tf_op jit(solution)/shard_map/finish/pallas_call | solution.py:837

commit v6 on v5

--- a/solution.py
+++ b/solution.py
@@ -162,7 +162,7 @@
     w_in, w_bias, w_out, vel, cot, along_y, smoothed, feats, gfeats, pulled,
     scalars, columns, tall, ztab,
     left_lhs, out_lhs, back_lhs, force_lhs, rhs, pulled_out, hidden_buf, pre_buf, sums,
-    x1_send, x1_recv, state, x2_send, x2_recv, x3_send, x3_recv, plane_send, plane_recv, plane_edge,
+    x1_send, x1_recv, state, group_rows, x2_send, x2_recv, x3_send, x3_recv, plane_send, plane_recv, plane_edge,
     y_send, y_recv, y_edge,
     p1, p2, p3,
     token, local_sem, x1_ss, x1_rs, x2_ss, x2_rs, x3_ss, x3_rs, plane_ss, plane_rs, edge_ss, edge_rs,
@@ -382,20 +382,25 @@
             jnp.where(lower, back_left, back_right),
         ]
 
-    def back_piece(ring_state, load, other, comp):
-        total = two_scalars(BACK_L + 5 * other, BACK_R + 5 * other) * ring_state[comp]
+    def group_part(load, other, comp):
+        total = jnp.zeros((8, 128), F32)
         for source in range(GROUP):
             index = 5 * other + 1 + source
             total = total + two_scalars(BACK_L + index, BACK_R + index) * load(source, comp)
         return total
 
-    def project(order, other, comp, tile):
-        out = sum(tall[24 * order + 8 + col] * tile[col:col + 1] for col in range(8))
+    def ring_factor(other):
+        return two_scalars(BACK_L + 5 * other, BACK_R + 5 * other)
+
+    def projected(order, tile):
+        return sum(tall[24 * order + 8 + col] * tile[col:col + 1] for col in range(8))
+
+    def keep_rows(order, other, comp, out):
         for kind in range(4):
             plane_send[order, other, kind // 2, kind % 2, comp:comp + 1, :] = out[kind:kind + 1]
 
-    def plane_rows_send(order):
-        for step in (2, 1, 3, 0):
+    def plane_rows_send(order, steps):
+        for step in steps:
             other = in_group(step)
             for along in (4, 5, 3, 6, 2, 7, 1):
                 place = in_line(along)
@@ -560,15 +565,22 @@
 
     lax.fori_loop(0, ROWS, grad_of_hidden, 0)
     wait_tokens(2, 1 + GROUP)
+    for other in range(GROUP):
+        for comp in range(3):
+            tile = group_part(first_piece, other, comp)
+            x3_send[0, other, comp] = tile
+            group_rows[other, comp] = projected(0, tile)
     ring_state = ring_receive(0)
-    for step in (2, 1, 3, 0):
+    ring_rows = [projected(0, ring_state[comp]) for comp in range(3)]
+    for step in range(GROUP):
         other = in_group(step)
-        for comp in range(3):
-            tile = back_piece(ring_state, first_piece, other, comp)
-            x3_send[0, other, comp] = tile
-            project(0, other, comp, tile)
-    plane_rows_send(0)
+        factor = ring_factor(other)
+        for comp in range(3):
+            x3_send[0, other, comp] += factor * ring_state[comp]
+            keep_rows(0, other, comp, group_rows[other, comp] + factor * ring_rows[comp])
+    plane_rows_send(0, (2,))
     pieces_send(x3_send, x3_recv, x3_ss, x3_rs, 0)
+    plane_rows_send(0, (1, 3, 0))
     x3_recv[0, member] = x3_send[0, member]
     pieces_wait(x3_send, x3_recv, x3_ss, x3_rs, 0)
     for comp in range(3):
@@ -580,11 +592,12 @@
         for row in range(ROWS):
             start = (comp * ROWS + row) * 8
             feats[row, 24 + 8 * comp:32 + 8 * comp, :] = along_z[start:start + 8]
+    for piece in range(GROUP):
+        for comp in range(3):
+            state[piece, comp] = own_block(0, x3_recv[0, piece, comp])
     plane_rows_wait(0)
     for comp in range(3):
-        left, right = unpack([
-            own_block(0, x3_recv[0, piece, comp]) + from_plane(0, piece, comp) for piece in range(GROUP)
-        ])
+        left, right = unpack([state[piece, comp] + from_plane(0, piece, comp) for piece in range(GROUP)])
         for row in range(ROWS):
             feats[row, 8 * comp:8 * comp + 8, :] += scalar(LEFT + row) * left + scalar(RIGHT + row) * right
 
@@ -613,8 +626,8 @@
         left, right = states([grad_along_y(comp, row) for row in range(ROWS)])
         for piece in range(GROUP):
             packed[piece, comp] = pack(left, right, piece)
-            project(1, piece, comp, packed[piece, comp])
-    plane_rows_send(1)
+            keep_rows(1, piece, comp, projected(1, packed[piece, comp]))
+    plane_rows_send(1, (2, 1, 3, 0))
     back_in = jnp.concatenate(
         [gfeats[row, 24 + 8 * comp:32 + 8 * comp, :] for comp in range(3) for row in range(ROWS)], axis=0
     )
@@ -726,14 +739,18 @@
         for row, value in enumerate(local_rows([pulled[comp, row] for row in range(ROWS)])):
             grad_velocity[comp, row] = cot[comp, row] + value
     sum_group()
+    for other in range(GROUP):
+        for comp in range(3):
+            x3_send[1, other, comp] = group_part(second_piece, other, comp)
     drain(early)
     plane_rows_drain(0)
     plane_rows_drain(1)
     ring_state = ring_receive(1)
-    for step in (2, 1, 3, 0):
+    for step in range(GROUP):
         other = in_group(step)
-        for comp in range(3):
-            x3_send[1, other, comp] = back_piece(ring_state, second_piece, other, comp)
+        factor = ring_factor(other)
+        for comp in range(3):
+            x3_send[1, other, comp] += factor * ring_state[comp]
     pieces_send(x3_send, x3_recv, x3_ss, x3_rs, 1)
     x3_recv[1, member] = x3_send[1, member]
     pieces_wait(x3_send, x3_recv, x3_ss, x3_rs, 1)
@@ -801,6 +818,7 @@
             pltpu.VMEM((88, 512), F32),
             pltpu.VMEM((2, GROUP, 3, 8, 128), F32),
             pltpu.VMEM((2, GROUP, 3, 8, 128), F32),
+            pltpu.VMEM((GROUP, 3, 8, 128), F32),
             pltpu.VMEM((GROUP, 3, 8, 128), F32),
             pltpu.VMEM((2, 2, 3, 4, 128), F32),
             pltpu.VMEM((2, RING, 3, 4, 128), F32),

time: 50.5 us -> 50.3 us (level)
  no operation moved by 1% of the time
where the time goes in v6:
time: 50.3 us; the launch traced here: 50.2 us
  Pallas kernels  49.5 us (98%)
  between operations  0.64 us (1%)
    pallas_call x1, Pallas kernels, local(): pl.pallas_call(kernel, out_shape=(pltpu.VMEM(field, F32), pltpu.VMEM(fiel...  48.2 us
    pallas_call x1, Pallas kernels, local(): pl.pallas_call(finish, out_shape=(jax.ShapeDtypeStruct(field, F32), jax.S...  1.29 us

profile of v6, /device:TPU:2, one launch (start us, length us, event | category | flops | bytes accessed | tf_op | source)
XLA Modules:
  0.0 50.2 jit_solution(8828902225176966473)
XLA Ops:
  0.6 48.2 %closure_step.1 = (f32[3,4,8,256]{3,2,1,0:T(8,128)S(1)}, f32[3,4,8,256]{3,2,1,0:T(8,128)S(1)}, f32[8,128]{1,0:T(8,128)S(1)}) custom-call(f32[3,4,8,256]{3,2,1,0:T(8,128)} %velocity.1, f32[3,4,8,256]{3,2,1,0:T(8,128)} %cotangent.1, f32[6,64]{1,0:T(8,128)} %weight_in.1, f32[1,64]{1,0:T(1,128)} %bitcast.5, f32[3,64]{1,0:T(4,128)} %bitcast.4, ...), custom_call_target="tpu_custom_call" | custom-call | tf_op jit(solution)/shard_map/closure_step/pallas_call | solution.py:786
  48.9 1.3 %finish.1 = (f32[3,4,8,256]{3,2,1,0:T(8,128)}, f32[3,4,8,256]{3,2,1,0:T(8,128)}, f32[6,64]{1,0:T(8,128)}, f32[1,64]{1,0:T(1,128)}, f32[3,64]{1,0:T(4,128)}) custom-call(f32[3,4,8,256]{3,2,1,0:T(8,128)S(1)} %get-tuple-element.13.new_velocity_in, f32[3,4,8,256]{3,2,1,0:T(8,128)S(1)} %get-tuple-element.14.grad_velocity_in, f32[8,128]{1,0:T(8,128)S(1)} %get-tuple-element.15.grads), custom_call_target="tpu_custom_call" | custom-call | tf_op jit(solution)/shard_map/finish/pallas_call | solution.py:855

commit v7 on v6

--- a/solution.py
+++ b/solution.py
@@ -762,18 +762,26 @@
     drain(len(sent))
 
 
-def finish(new_velocity_in, grad_velocity_in, grads, new_velocity, grad_velocity, grad_in, grad_bias, grad_out_t, sems):
+def finish(
+    new_velocity_in, grad_velocity_in, grads, new_velocity, grad_velocity, grad_in, grad_bias, grad_out_t,
+    small_in, small_bias, small_out, sems,
+):
     copies = [
-        pltpu.make_async_copy(new_velocity_in, new_velocity, sems.at[0]),
-        pltpu.make_async_copy(grad_velocity_in, grad_velocity, sems.at[1]),
+        pltpu.make_async_copy(source.at[comp], target.at[comp], sems.at[2 * comp + place])
+        for comp in range(3)
+        for place, (source, target) in enumerate(((new_velocity_in, new_velocity), (grad_velocity_in, grad_velocity)))
     ]
     for copy in copies:
         copy.start()
     front = grads[:, 0:UNITS]
-    grad_in[...] = front[0:6]
-    grad_bias[...] = front[6:7]
-    grad_out_t[0:1] = front[7:8]
-    grad_out_t[1:3] = grads[0:2, UNITS:2 * UNITS]
+    small_in[...] = front[0:6]
+    small_bias[...] = front[6:7]
+    small_out[0:1] = front[7:8]
+    small_out[1:3] = grads[0:2, UNITS:2 * UNITS]
+    small = ((small_in, grad_in), (small_bias, grad_bias), (small_out, grad_out_t))
+    for place, (source, target) in enumerate(small):
+        copies.append(pltpu.make_async_copy(source, target, sems.at[6 + place]))
+        copies[-1].start()
     for copy in copies:
         copy.wait()
 
@@ -862,8 +870,13 @@
             jax.ShapeDtypeStruct((3, UNITS), F32),
         ),
         in_specs=[whole] * 3,
-        out_specs=(anywhere, anywhere, whole, whole, whole),
-        scratch_shapes=[dma((2,))],
+        out_specs=(anywhere,) * 5,
+        scratch_shapes=[
+            pltpu.VMEM((6, UNITS), F32),
+            pltpu.VMEM((1, UNITS), F32),
+            pltpu.VMEM((3, UNITS), F32),
+            dma((9,)),
+        ],
         compiler_params=pltpu.CompilerParams(vmem_limit_bytes=1 << 20),
         name="finish",
     )(*mid)

time: 50.3 us -> 49.8 us (0.990)
    pallas_call x1, Pallas kernels: 1.29 us -> 0.76 us  [local(): pl.pallas_call(finish, out_shape=(jax.ShapeDtypeStruct(field, F32), jax.S...]
where the time goes in v7:
time: 49.8 us; the launch traced here: 49.6 us
  Pallas kernels  49 us (98%)
  between operations  0.64 us (1%)
    pallas_call x1, Pallas kernels, local(): pl.pallas_call(kernel, out_shape=(pltpu.VMEM(field, F32), pltpu.VMEM(fiel...  48.2 us

profile of v7, /device:TPU:2, one launch (start us, length us, event | category | flops | bytes accessed | tf_op | source)
XLA Modules:
  0.0 49.6 jit_solution(15174477839891119802)
XLA Ops:
  0.6 48.2 %closure_step.1 = (f32[3,4,8,256]{3,2,1,0:T(8,128)S(1)}, f32[3,4,8,256]{3,2,1,0:T(8,128)S(1)}, f32[8,128]{1,0:T(8,128)S(1)}) custom-call(f32[3,4,8,256]{3,2,1,0:T(8,128)} %velocity.1, f32[3,4,8,256]{3,2,1,0:T(8,128)} %cotangent.1, f32[6,64]{1,0:T(8,128)} %weight_in.1, f32[1,64]{1,0:T(1,128)} %bitcast.5, f32[3,64]{1,0:T(4,128)} %bitcast.4, ...), custom_call_target="tpu_custom_call" | custom-call | tf_op jit(solution)/shard_map/closure_step/pallas_call | solution.py:794
  48.9 0.8 %finish.1 = (f32[3,4,8,256]{3,2,1,0:T(8,128)}, f32[3,4,8,256]{3,2,1,0:T(8,128)}, f32[6,64]{1,0:T(8,128)}, f32[1,64]{1,0:T(1,128)}, f32[3,64]{1,0:T(4,128)}) custom-call(f32[3,4,8,256]{3,2,1,0:T(8,128)S(1)} %get-tuple-element.13.new_velocity_in, f32[3,4,8,256]{3,2,1,0:T(8,128)S(1)} %get-tuple-element.14.grad_velocity_in, f32[8,128]{1,0:T(8,128)S(1)} %get-tuple-element.15.grads), custom_call_target="tpu_custom_call" | custom-call | tf_op jit(solution)/shard_map/finish/pallas_call | solution.py:863

commit v8 on v7

--- a/solution.py
+++ b/solution.py
@@ -527,9 +527,9 @@
         left, right = states([vel[comp, row] for row in range(ROWS)])
         for piece in range(GROUP):
             x1_send[0, piece, comp] = pack(left, right, piece)
-    build_columns()
     pass_tokens()
     pieces_send(x1_send, x1_recv, x1_ss, x1_rs, 0)
+    build_columns()
     line_send(lambda comp, row: vel[comp, row], 0)
     x1_recv[0, member] = x1_send[0, member]
     build_weights()
@@ -627,7 +627,7 @@
         for piece in range(GROUP):
             packed[piece, comp] = pack(left, right, piece)
             keep_rows(1, piece, comp, projected(1, packed[piece, comp]))
-    plane_rows_send(1, (2, 1, 3, 0))
+    plane_rows_send(1, (2, 1, 3))
     back_in = jnp.concatenate(
         [gfeats[row, 24 + 8 * comp:32 + 8 * comp, :] for comp in range(3) for row in range(ROWS)], axis=0
     )
@@ -640,6 +640,7 @@
         for row in range(ROWS):
             pulled[comp, row] = along_z[starts[row]:starts[row] + 8]
     pieces_send(x1_send, x1_recv, x1_ss, x1_rs, 1)
+    plane_rows_send(1, (0,))
     x1_recv[1, member] = x1_send[1, member]
 
     def keep_pulled(comp, row, value):
@@ -753,6 +754,7 @@
             x3_send[1, other, comp] += factor * ring_state[comp]
     pieces_send(x3_send, x3_recv, x3_ss, x3_rs, 1)
     x3_recv[1, member] = x3_send[1, member]
+    drain(RING - 1 + GROUP - 1)
     pieces_wait(x3_send, x3_recv, x3_ss, x3_rs, 1)
     for comp in range(3):
         left, right = unpack([x3_recv[1, piece, comp] for piece in range(GROUP)])

time: 49.8 us -> 49.7 us (level)
  no operation moved by 1% of the time
where the time goes in v8:
time: 49.7 us; the launch traced here: 49.6 us
  Pallas kernels  49 us (99%)
  between operations  0.64 us (1%)
    pallas_call x1, Pallas kernels, local(): pl.pallas_call(kernel, out_shape=(pltpu.VMEM(field, F32), pltpu.VMEM(fiel...  48.2 us

profile of v8, /device:TPU:2, one launch (start us, length us, event | category | flops | bytes accessed | tf_op | source)
XLA Modules:
  0.0 49.6 jit_solution(3549627225184075137)
XLA Ops:
  0.6 48.2 %closure_step.1 = (f32[3,4,8,256]{3,2,1,0:T(8,128)S(1)}, f32[3,4,8,256]{3,2,1,0:T(8,128)S(1)}, f32[8,128]{1,0:T(8,128)S(1)}) custom-call(f32[3,4,8,256]{3,2,1,0:T(8,128)} %velocity.1, f32[3,4,8,256]{3,2,1,0:T(8,128)} %cotangent.1, f32[6,64]{1,0:T(8,128)} %weight_in.1, f32[1,64]{1,0:T(1,128)} %bitcast.5, f32[3,64]{1,0:T(4,128)} %bitcast.4, ...), custom_call_target="tpu_custom_call" | custom-call | tf_op jit(solution)/shard_map/closure_step/pallas_call | solution.py:796
  48.9 0.8 %finish.1 = (f32[3,4,8,256]{3,2,1,0:T(8,128)}, f32[3,4,8,256]{3,2,1,0:T(8,128)}, f32[6,64]{1,0:T(8,128)}, f32[1,64]{1,0:T(1,128)}, f32[3,64]{1,0:T(4,128)}) custom-call(f32[3,4,8,256]{3,2,1,0:T(8,128)S(1)} %get-tuple-element.13.new_velocity_in, f32[3,4,8,256]{3,2,1,0:T(8,128)S(1)} %get-tuple-element.14.grad_velocity_in, f32[8,128]{1,0:T(8,128)S(1)} %get-tuple-element.15.grads), custom_call_target="tpu_custom_call" | custom-call | tf_op jit(solution)/shard_map/finish/pallas_call | solution.py:865
